TPU v7x, 32 devices: a whole 2x2x4 slice. The times are simulated.
32 devices in a mesh: groups: 2 (over y), seq: 4 (over z), tile: 2 (over x), chan: 2 (over core).
Axes of the slice: x: 2, y: 2, z: 4, core: 2. Of those that a mesh axis runs over, the one named last changes fastest.
Arguments:
- latents: bfloat16 [2, 7680, 384], P('tile', ('groups', 'seq'), 'chan'), parts along dimension 1, may hold values from -6 to 6
- norm_gain: float32 [384], replicated, may hold values from 0.1 to 1.9
- conv_weight: bfloat16 [3, 3, 3, 384, 384], P(None, None, None, None, 'chan'), may hold values from -0.0625 to 0.0625
- conv_bias: float32 [384], P('chan'), may hold values from -3 to 3
- upsample_weight: bfloat16 [3, 3, 384, 192], P(None, None, None, 'chan'), may hold values from -0.109375 to 0.109375
- upsample_bias: float32 [192], P('chan'), may hold values from -3 to 3
Outputs:
- decoded: bfloat16 [8, 192, 20, 384], P(None, ('groups', 'tile'), 'seq', 'chan'), parts along dimension 1
There are 2 independent parts, one for each index of `groups`. A program takes and returns all parts, laid end to end along the dimension named above; an argument that names none is the same for every part. Nothing has to cross between parts.
All inputs are finite; a program needn't handle non-finite values.
Results may differ from a plain program's by a relative error of at most 0.005.
Values may be sent and summed in bfloat16 or wider, within the bound.
No kernel may reach another device: no remote copies, remote signals or barrier semaphores. Data moves between devices by JAX's collectives and lax.ppermute only.
A program may use at most 64 MiB of HBM per device.

v0:
```python
import jax
import jax.numpy as jnp
from jax import lax
from jax.sharding import PartitionSpec as P

FRAMES = 8
ROWS_DEV = 24
COLS_DEV = 5


norm_eps = 1e-06


def extended(cells, sides, width):
    for axis, dim in sides:
        count = lax.axis_size(axis)
        ends = count - 1
        head = lax.slice_in_dim(cells, 0, width, axis=dim)
        tail = lax.slice_in_dim(cells, cells.shape[dim] - width, cells.shape[dim], axis=dim)
        cells = jnp.concatenate(
            [
                lax.ppermute(tail, axis, [(i, (i + 1) % count) for i in range(ends)]),
                cells,
                lax.ppermute(head, axis, [((i + 1) % count, i) for i in range(ends)]),
            ],
            axis=dim,
        )
    return cells


def activate(padded, norm_gain):
    values = padded.astype(jnp.float32)
    scale = lax.rsqrt(jnp.mean(values * values, axis=-1, keepdims=True) + norm_eps)
    return jax.nn.silu(values * scale * norm_gain).astype(jnp.bfloat16)


def body(latents, norm_gain, conv_weight, conv_bias, upsample_weight, upsample_bias):
    seq_count = lax.axis_size("seq")
    local_chan = conv_bias.shape[0]
    rows_src = FRAMES * ROWS_DEV // seq_count
    whole = lax.all_gather(latents[0], "chan", axis=1, tiled=True)
    arranged = whole.reshape(rows_src, seq_count, COLS_DEV, whole.shape[1])
    regrouped = lax.all_to_all(arranged, "seq", split_axis=1, concat_axis=0, tiled=True)
    full_field = regrouped.reshape(FRAMES, ROWS_DEV, COLS_DEV, whole.shape[1])
    padded = extended(full_field, (("seq", 2), ("tile", 1)), 1)
    field_own = lax.dynamic_slice_in_dim(
        full_field, lax.axis_index("chan") * local_chan, local_chan, 3
    )
    activation = activate(padded, norm_gain)
    shifted = jnp.pad(activation, ((2, 0), (0, 0), (0, 0), (0, 0)))
    conv_out = lax.conv_general_dilated(
        shifted[None],
        conv_weight,
        (1, 1, 1),
        "VALID",
        dimension_numbers=("NDHWC", "DHWIO", "NDHWC"),
        preferred_element_type=jnp.float32,
    )[0]
    middle = (field_own.astype(jnp.float32) + conv_out + conv_bias).astype(jnp.bfloat16)
    middle_rim = extended(middle, (("seq", 2), ("tile", 1)), 1)
    middle_full = lax.all_gather(middle_rim, "chan", axis=3, tiled=True)
    upsampled = jnp.repeat(jnp.repeat(middle_full, 2, axis=1), 2, axis=2)[:, 1:-1, 1:-1, :]
    image = lax.conv_general_dilated(
        upsampled,
        upsample_weight,
        (1, 1),
        "VALID",
        dimension_numbers=("NHWC", "HWIO", "NHWC"),
        preferred_element_type=jnp.float32,
    )
    image = image + upsample_bias
    out_chan = upsample_bias.shape[0]
    image = image.reshape(FRAMES, 2 * ROWS_DEV, COLS_DEV, 2, out_chan)
    image = jnp.transpose(image, (0, 1, 2, 4, 3)).reshape(
        FRAMES, 2 * ROWS_DEV, COLS_DEV, 2 * out_chan
    )
    return image.astype(jnp.bfloat16)


def solution(mesh):
    in_specs = (
        P("tile", ("groups", "seq"), "chan"),
        P(),
        P(None, None, None, None, "chan"),
        P("chan"),
        P(None, None, None, "chan"),
        P("chan"),
    )
    out_specs = P(None, ("groups", "tile"), "seq", "chan")
    return jax.shard_map(body, mesh=mesh, in_specs=in_specs, out_specs=out_specs, check_vma=False)
```

profile of v0, /device:TPU:0, one launch (start us, length us, event | category | flops | bytes accessed | tf_op | source)
XLA Modules:
  0.0 154.0 jit_solution(12144148786594133457)
XLA Ops:
  6.5 2.8 %all-gather = bf16[1,960,384]{1,2,0:T(8,128)(2,1)S(1)} all-gather(bf16[1,960,192]{1,2,0:T(8,128)(2,1)} %param.6), channel_id=2, replica_groups=mesh['groups'=2,'seq'=4,'tile'=2,'chan'=2] {'chan'}, dimensions={2}, use_global_device_ids=true | all-gather | bytes 1105920 | tf_op jit(solution)/shard_map/all_gather | solution.py:41
  9.4 0.4 copy.26
  9.7 0.3 reshape.28
  10.3 25.4 %all_to_all.15 = bf16[48,4,5,384]{3,0,2,1:T(8,128)(2,1)S(1)} all-to-all(bf16[48,4,5,384]{3,0,2,1:T(8,128)(2,1)S(1)} %copy.27), channel_id=1, replica_groups=mesh['groups'=2,'seq'=4,'tile'=2,'chan'=2] {'seq'}, dimensions={1} | all-to-all | bytes 1474560 | tf_op jit(solution)/shard_map/all_to_all | solution.py:43
  35.8 2.3 %collective-permute-start = (bf16[8,24,1,384]{3,1,0,2:T(8,128)(2,1)S(1)}, bf16[8,24,1,384]{3,1,0,2:T(8,128)(2,1)S(1)}, u32[]{:S(2)}, u32[]{:S(2)}) collective-permute-start(bf16[8,24,1,384]{3,1,0,2:T(8,128)(2,1)S(1)} %get-tuple-element.7), channel_id=1, source_target_pairs={{0,4},{4,8},{8,12},{1,5},{5,9},{9,13},{2,6},{6,10},{10,14},{3,7},{... | collective-permute-start | bytes 442376 | tf_op jit(solution)/shard_map/ppermute | solution.py:22
  38.1 1.3 collective-permute-start.1
  39.4 1.3 collective-permute-done
  40.7 4.4 %collective-permute-done.1 = bf16[8,24,1,384]{3,1,0,2:T(8,128)(2,1)S(1)} collective-permute-done((bf16[8,24,1,384]{3,1,0,2:T(8,128)(2,1)S(1)}, bf16[8,24,1,384]{3,1,0,2:T(8,128)(2,1)S(1)}, u32[]{:S(2)}, u32[]{:S(2)}) %collective-permute-start.1) | collective-permute-done | bytes 147488 | tf_op jit(solution)/shard_map/ppermute | solution.py:24
  45.3 3.4 %collective-permute-start.2 = (bf16[8,1,7,384]{3,1,0,2:T(2,128)(2,1)S(1)}, bf16[8,1,7,384]{3,1,0,2:T(2,128)(2,1)S(1)}, u32[]{:S(2)}, u32[]{:S(2)}) collective-permute-start(bf16[8,1,7,384]{3,1,0,2:T(2,128)(2,1)S(1)} %get-tuple-element.5), channel_id=1, source_target_pairs={{0,2},{1,3},{4,6},{5,7},{8,10},{9,11},{12,14},{13,15},{16,18},{17,... | collective-permute-start | bytes 129032 | tf_op jit(solution)/shard_map/ppermute | solution.py:22
  48.7 1.3 collective-permute-start.3
  50.0 0.8 collective-permute-done.2
  50.8 4.3 %collective-permute-done.3 = bf16[8,1,7,384]{3,1,0,2:T(2,128)(2,1)S(1)} collective-permute-done((bf16[8,1,7,384]{3,1,0,2:T(2,128)(2,1)S(1)}, bf16[8,1,7,384]{3,1,0,2:T(2,128)(2,1)S(1)}, u32[]{:S(2)}, u32[]{:S(2)}) %collective-permute-start.3) | collective-permute-done | bytes 43040 | tf_op jit(solution)/shard_map/ppermute | solution.py:24
  55.1 0.7 fusion.2
  55.8 1.5 fusion.9
  57.6 0.4 copy-done.3
  57.9 29.8 %fusion = f32[1,8,24,5,192]{4,0,3,2,1:T(1,128)S(1)} fusion(bf16[3,3,3,384,192]{3,4,2,1,0:T(8,128)(2,1)S(1)} %copy-done.3, bf16[1,10,26,7,384]{4,2,1,3,0:T(8,128)(2,1)S(1)} %pad_bitcast_fusion), kind=kOutput, calls=%fused_computation.2 | convolution fusion | flops 3822059520 | bytes 6116352 | tf_op jit(solution)/shard_map/conv_general_dilated | solution.py:51
  88.0 2.5 %collective-permute-start.4 = (bf16[8,24,1,192]{3,1,0,2:T(8,128)(2,1)S(1)}, bf16[8,24,1,192]{3,1,0,2:T(8,128)(2,1)S(1)}, u32[]{:S(2)}, u32[]{:S(2)}) collective-permute-start(bf16[8,24,1,192]{3,1,0,2:T(8,128)(2,1)S(1)} %get-tuple-element.11), channel_id=1, source_target_pairs={{0,4},{4,8},{8,12},{1,5},{5,9},{9,13},{2,6},{6,10},{10,14},{3,7},{... | collective-permute-start | bytes 221192 | tf_op jit(solution)/shard_map/ppermute | solution.py:22
  90.5 1.3 collective-permute-start.5
  91.8 0.9 collective-permute-done.4
  92.7 4.3 %collective-permute-done.5 = bf16[8,24,1,192]{3,1,0,2:T(8,128)(2,1)S(1)} collective-permute-done((bf16[8,24,1,192]{3,1,0,2:T(8,128)(2,1)S(1)}, bf16[8,24,1,192]{3,1,0,2:T(8,128)(2,1)S(1)}, u32[]{:S(2)}, u32[]{:S(2)}) %collective-permute-start.5) | collective-permute-done | bytes 73760 | tf_op jit(solution)/shard_map/ppermute | solution.py:24
  97.1 1.5 %collective-permute-start.6 = (bf16[8,1,7,192]{3,1,0,2:T(2,128)(2,1)S(1)}, bf16[8,1,7,192]{3,1,0,2:T(2,128)(2,1)S(1)}, u32[]{:S(2)}, u32[]{:S(2)}) collective-permute-start(bf16[8,1,7,192]{3,1,0,2:T(2,128)(2,1)S(1)} %get-tuple-element.9), channel_id=1, source_target_pairs={{0,2},{1,3},{4,6},{5,7},{8,10},{9,11},{12,14},{13,15},{16,18},{17,... | collective-permute-start | bytes 64520 | tf_op jit(solution)/shard_map/ppermute | solution.py:22
  98.7 1.3 collective-permute-start.7
  100.0 0.5 collective-permute-done.6
  100.5 4.3 %collective-permute-done.7 = bf16[8,1,7,192]{3,1,0,2:T(2,128)(2,1)S(1)} collective-permute-done((bf16[8,1,7,192]{3,1,0,2:T(2,128)(2,1)S(1)}, bf16[8,1,7,192]{3,1,0,2:T(2,128)(2,1)S(1)}, u32[]{:S(2)}, u32[]{:S(2)}) %collective-permute-start.7) | collective-permute-done | bytes 21536 | tf_op jit(solution)/shard_map/ppermute | solution.py:24
  104.8 0.5 pad_maximum_fusion.1
  105.3 3.5 %copy.33 = bf16[8,26,7,192]{1,0,2,3:T(8,128)(2,1)} copy(bf16[8,26,7,192]{3,1,0,2:T(8,128)(2,1)S(1)} %pad_maximum_fusion.1) | data formatting | bytes 1118208 | tf_op jit(solution)/shard_map/concatenate | solution.py:20
  108.8 14.2 %all-gather.3.cloned.1.call-done = bf16[8,26,7,384]{1,0,2,3:T(8,128)(2,1)} async-done(((bf16[8,26,7,192]{1,0,2,3:T(8,128)(2,1)}), bf16[8,26,7,384]{1,0,2,3:T(8,128)(2,1)}) %all-gather.3.cloned.1.call-update) | async-done | bytes 1118224 | tf_op jit(solution)/shard_map/all_gather | solution.py:61
  122.9 9.9 %copy.34 = bf16[8,26,7,384]{3,0,2,1:T(8,128)(2,1)S(1)} copy(bf16[8,26,7,384]{1,0,2,3:T(8,128)(2,1)} %all-gather.3.cloned.1.call-done) | data formatting | bytes 2236416 | tf_op jit(solution)/shard_map/all_gather | solution.py:61
  133.1 0.4 broadcast_in_dim.15
  133.7 8.0 %add_convert_fusion = bf16[8,48,10,96]{3,0,2,1:T(8,128)(2,1)} fusion(bf16[8,52,14,384]{3,0,2,1:T(8,128)(2,1)S(1)} %bitcast.30, bf16[3,3,384,96]{2,3,1,0:T(8,128)(2,1)S(1)} %copy-done, f32[96]{0:T(128)S(1)} %copy-done.4), kind=kOutput, calls=%fused_computation.12 | convolution fusion | flops 2548776960 | bytes 5874048 | tf_op jit(solution)/shard_map/conv_general_dilated | solution.py:63
  141.7 2.6 %copy.35 = bf16[8,48,5,2,96]{1,0,3,4,2:T(8,128)(2,1)S(1)} copy(bf16[8,48,5,2,96]{4,0,3,2,1:T(8,128)(2,1)} %bitcast.31) | data formatting | bytes 1474560 | tf_op jit(solution)/shard_map/convert_element_type | solution.py:77
  144.4 2.8 %copy.36 = bf16[8,48,5,192]{3,1,2,0:T(8,128)(2,1)} copy(bf16[8,48,5,192]{1,0,3,2:T(8,128)(2,1)S(1)} %bitcast.29) | data formatting | bytes 1474560 | tf_op jit(solution)/shard_map/convert_element_type | solution.py:77
  (21 shorter events, 1.6 us)
Async XLA Ops:
  6.5 126.9 %copy-start = (bf16[3,3,384,96]{2,3,1,0:T(8,128)(2,1)S(1)}, bf16[3,3,384,96]{2,3,1,0:T(8,128)(2,1)}, u32[]{:S(2)}) copy-start(bf16[3,3,384,96]{2,3,1,0:T(8,128)(2,1)} %param.10) | copy-start | bytes 1990660
  6.5 116.4 %all-gather.3.cloned.1.call-start = ((), (), s32[]{:S(2)}) async-start(), calls=%async_computation.1 | async-start | bytes 8257536 | tf_op jit(solution)/shard_map/all_gather | solution.py:61
  10.3 45.5 %copy-start.1 = (f32[384]{0:T(512)S(1)}, f32[384]{0:T(512)}, u32[]{:S(2)}) copy-start(f32[384]{0:T(512)} %param.7) | copy-start | bytes 4612
  35.8 4.9 %collective-permute-start = (bf16[8,24,1,384]{3,1,0,2:T(8,128)(2,1)S(1)}, bf16[8,24,1,384]{3,1,0,2:T(8,128)(2,1)S(1)}, u32[]{:S(2)}, u32[]{:S(2)}) collective-permute-start(bf16[8,24,1,384]{3,1,0,2:T(8,128)(2,1)S(1)} %get-tuple-element.7), channel_id=1, source_target_pairs={{0,4},{4,8},{8,12},{1,5},{5,9},{9,13},{2,6},{6,10},{10,14},{3,7},{... | collective-permute-start | bytes 442376 | tf_op jit(solution)/shard_map/ppermute | solution.py:22
  38.1 7.0 %collective-permute-start.1 = (bf16[8,24,1,384]{3,1,0,2:T(8,128)(2,1)S(1)}, bf16[8,24,1,384]{3,1,0,2:T(8,128)(2,1)S(1)}, u32[]{:S(2)}, u32[]{:S(2)}) collective-permute-start(bf16[8,24,1,384]{3,1,0,2:T(8,128)(2,1)S(1)} %get-tuple-element.8), channel_id=1, source_target_pairs={{4,0},{8,4},{12,8},{5,1},{9,5},{13,9},{6,2},{10,6},{14,10},{7,3},{... | collective-permute-start | bytes 442376 | tf_op jit(solution)/shard_map/ppermute | solution.py:24
  45.3 5.5 %collective-permute-start.2 = (bf16[8,1,7,384]{3,1,0,2:T(2,128)(2,1)S(1)}, bf16[8,1,7,384]{3,1,0,2:T(2,128)(2,1)S(1)}, u32[]{:S(2)}, u32[]{:S(2)}) collective-permute-start(bf16[8,1,7,384]{3,1,0,2:T(2,128)(2,1)S(1)} %get-tuple-element.5), channel_id=1, source_target_pairs={{0,2},{1,3},{4,6},{5,7},{8,10},{9,11},{12,14},{13,15},{16,18},{17,... | collective-permute-start | bytes 129032 | tf_op jit(solution)/shard_map/ppermute | solution.py:22
  48.7 6.4 %collective-permute-start.3 = (bf16[8,1,7,384]{3,1,0,2:T(2,128)(2,1)S(1)}, bf16[8,1,7,384]{3,1,0,2:T(2,128)(2,1)S(1)}, u32[]{:S(2)}, u32[]{:S(2)}) collective-permute-start(bf16[8,1,7,384]{3,1,0,2:T(2,128)(2,1)S(1)} %get-tuple-element.6), channel_id=1, source_target_pairs={{2,0},{3,1},{6,4},{7,5},{10,8},{11,9},{14,12},{15,13},{18,16},{19,... | collective-permute-start | bytes 129032 | tf_op jit(solution)/shard_map/ppermute | solution.py:24
  55.8 2.1 %copy-start.3 = (bf16[3,3,3,384,192]{3,4,2,1,0:T(8,128)(2,1)S(1)}, bf16[3,3,3,384,192]{3,4,2,1,0:T(8,128)(2,1)}, u32[]{:S(2)}) copy-start(bf16[3,3,3,384,192]{3,4,2,1,0:T(8,128)(2,1)} %param.8) | copy-start | bytes 11943940
  57.9 29.8 %copy-start.2 = (f32[192]{0:T(256)S(1)}, f32[192]{0:T(256)}, u32[]{:S(2)}) copy-start(f32[192]{0:T(256)} %param.9) | copy-start | bytes 2308
  88.0 4.7 %collective-permute-start.4 = (bf16[8,24,1,192]{3,1,0,2:T(8,128)(2,1)S(1)}, bf16[8,24,1,192]{3,1,0,2:T(8,128)(2,1)S(1)}, u32[]{:S(2)}, u32[]{:S(2)}) collective-permute-start(bf16[8,24,1,192]{3,1,0,2:T(8,128)(2,1)S(1)} %get-tuple-element.11), channel_id=1, source_target_pairs={{0,4},{4,8},{8,12},{1,5},{5,9},{9,13},{2,6},{6,10},{10,14},{3,7},{... | collective-permute-start | bytes 221192 | tf_op jit(solution)/shard_map/ppermute | solution.py:22
  90.5 6.5 %collective-permute-start.5 = (bf16[8,24,1,192]{3,1,0,2:T(8,128)(2,1)S(1)}, bf16[8,24,1,192]{3,1,0,2:T(8,128)(2,1)S(1)}, u32[]{:S(2)}, u32[]{:S(2)}) collective-permute-start(bf16[8,24,1,192]{3,1,0,2:T(8,128)(2,1)S(1)} %get-tuple-element.12), channel_id=1, source_target_pairs={{4,0},{8,4},{12,8},{5,1},{9,5},{13,9},{6,2},{10,6},{14,10},{7,3},{... | collective-permute-start | bytes 221192 | tf_op jit(solution)/shard_map/ppermute | solution.py:24
  97.1 3.4 %collective-permute-start.6 = (bf16[8,1,7,192]{3,1,0,2:T(2,128)(2,1)S(1)}, bf16[8,1,7,192]{3,1,0,2:T(2,128)(2,1)S(1)}, u32[]{:S(2)}, u32[]{:S(2)}) collective-permute-start(bf16[8,1,7,192]{3,1,0,2:T(2,128)(2,1)S(1)} %get-tuple-element.9), channel_id=1, source_target_pairs={{0,2},{1,3},{4,6},{5,7},{8,10},{9,11},{12,14},{13,15},{16,18},{17,... | collective-permute-start | bytes 64520 | tf_op jit(solution)/shard_map/ppermute | solution.py:22
  98.7 6.1 %collective-permute-start.7 = (bf16[8,1,7,192]{3,1,0,2:T(2,128)(2,1)S(1)}, bf16[8,1,7,192]{3,1,0,2:T(2,128)(2,1)S(1)}, u32[]{:S(2)}, u32[]{:S(2)}) collective-permute-start(bf16[8,1,7,192]{3,1,0,2:T(2,128)(2,1)S(1)} %get-tuple-element.10), channel_id=1, source_target_pairs={{2,0},{3,1},{6,4},{7,5},{10,8},{11,9},{14,12},{15,13},{18,16},{19,... | collective-permute-start | bytes 64520 | tf_op jit(solution)/shard_map/ppermute | solution.py:24
  133.1 0.7 copy-start.4
Sparse Core Ops, SparseCore 0:
  108.9 13.9 all-gather.2
where the time goes:
time: 154 us
  matrix products  37.8 us (25%)
  waiting for transfers between devices  35 us (23%)
  blocking collectives  28.2 us (18%)
  local copies, waits for them, and re-layouts  21.3 us (14%)
  starting transfers between devices  14.8 us (10%)
  between operations  13.6 us (9%)
  other arithmetic  3.28 us (2%)
    conv_general_dilated x1, matrix products, body(): lax.conv_general_dilated(shifted[None], conv_weight, (1, 1, 1), 'VALID',...  29.8 us
    all_to_all x1, blocking collectives, body(): lax.all_to_all(arranged, 'seq', split_axis=1, concat_axis=0, tiled=True)  25.4 us
    ppermute x4, waiting for transfers between devices, extended(): lax.ppermute(head, axis, [((i + 1) % count, i) for i in range(ends)])  17.3 us
    all_gather x1, waiting for transfers between devices, body(): middle_full = lax.all_gather(middle_rim, 'chan', axis=3, tiled=True)  14.2 us
    all_gather x1, local copies, waits for them, and re-layouts, body(): middle_full = lax.all_gather(middle_rim, 'chan', axis=3, tiled=True)  9.9 us
    ppermute x4, starting transfers between devices, extended(): lax.ppermute(tail, axis, [(i, (i + 1) % count) for i in range(ends)])  9.67 us
    conv_general_dilated x1, matrix products, body(): lax.conv_general_dilated(upsampled, upsample_weight, (1, 1), 'VALID', dim...  8.02 us
    convert_element_type x2, local copies, waits for them, and re-layouts, body(): return image.astype(jnp.bfloat16)  5.44 us
  transfers between devices with their start and end apart: 9, of which 9 were waited for; matrix products, arithmetic and copies ran while one was open for 0% of the time, Pallas kernels for 0%

commit v1 on v0

v1 whole, which is shorter than its diff:
```python
import functools

import jax
import jax.numpy as jnp
from jax import lax
from jax.experimental import pallas as pl
from jax.experimental.pallas import tpu as pltpu
from jax.sharding import PartitionSpec as P

FRAMES = 8
ROWS_DEV = 24
PAIRS = FRAMES // 2
PITCH = 32
HEAD = 8

norm_eps = 1e-06
f32 = jnp.float32
bf16 = jnp.bfloat16
VM = pl.BlockSpec(memory_space=pltpu.VMEM)
ANY = pl.BlockSpec(memory_space=pl.ANY)
MIB = 1024 * 1024


def dot_nt(a, b):
    return lax.dot_general(a, b, (((1,), (1,)), ((), ())), preferred_element_type=f32)


def call(kernel, out_shape, in_specs, out_specs, scratch, limit, name, flops=0, moved=0, aliases=None):
    return pl.pallas_call(
        kernel,
        out_shape=out_shape,
        in_specs=in_specs,
        out_specs=out_specs,
        scratch_shapes=list(scratch),
        compiler_params=pltpu.CompilerParams(vmem_limit_bytes=limit * MIB),
        input_output_aliases=aliases or {},
        cost_estimate=pl.CostEstimate(flops=flops, bytes_accessed=moved, transcendentals=0),
        name=name,
    )


def round_up(n, k):
    return -(-n // k) * k


def border_rows(width):
    return round_up(2 * width, 8)


def edge_kernel(span, colors, x_ref, *outs):
    tile = lax.axis_index("tile")
    half = ROWS_DEV * span
    seg = round_up(2 * span, 64)
    chan = x_ref.shape[0]
    for color in range(colors):
        below = lax.rem(tile + color, 2) == 0
        parts = []
        for p in range(2):
            last = x_ref[:, (p + 1) * half - 2 * span : (p + 1) * half]
            first = x_ref[:, p * half : p * half + 2 * span]
            parts += [jnp.where(below, last, first), jnp.zeros((chan, seg - 2 * span), bf16)]
        outs[color][...] = jnp.concatenate(parts, axis=1)


def selection(rows, per_col, width, cols, span, dest, tokens):
    r = lax.broadcasted_iota(jnp.int32, (rows, 1), 0)
    w = jnp.zeros_like(r)
    for k in range(1, width):
        w = w + (r >= k * per_col).astype(jnp.int32)
    h = r - w * per_col
    col = dest * cols - 2 + w
    good = (col >= 0) & (col < span) & (r < width * per_col)
    token = jnp.where(good, h * span + col, -1)
    lane = lax.broadcasted_iota(jnp.int32, (rows, tokens), 1)
    return jnp.where(lane == token, 1.0, 0.0).astype(bf16)


def pack_kernel(count, cols, x_ref, *outs):
    seq = lax.axis_index("seq")
    width, span = cols + 4, count * cols
    half = ROWS_DEV * span
    parts = [x_ref[:, p * half : (p + 1) * half] for p in range(2)]
    for d in range(count):
        dest = lax.rem(seq + d, count)
        pick = selection(width * ROWS_DEV, ROWS_DEV, width, cols, span, dest, half)
        both = jnp.concatenate([dot_nt(pick, part) for part in parts], axis=1)
        outs[d][0 : width * ROWS_DEV, :] = both.astype(bf16)


def border_kernel(count, cols, colors, *refs):
    edges = refs[:colors]
    outs = refs[colors + count : colors + 2 * count]
    held, sems = refs[colors + 2 * count :]
    seq = lax.axis_index("seq")
    width, span = cols + 4, count * cols
    rows = border_rows(width)
    seg = round_up(2 * span, 64)
    copies = []
    for d in range(count):
        dest = lax.rem(seq + d, count)
        pick = selection(rows, 2, width, cols, span, dest, seg)
        for color in range(colors):
            x = edges[color][...]
            both = jnp.concatenate([dot_nt(pick, x[:, p * seg : (p + 1) * seg]) for p in range(2)], axis=1)
            held[d, color * rows : (color + 1) * rows, :] = both.astype(bf16)
        to = outs[d].at[pl.ds(width * ROWS_DEV, colors * rows)]
        copies.append(pltpu.make_async_copy(held.at[d], to, sems.at[d]))
        copies[-1].start()
    for copy in copies:
        copy.wait()


def conv_kernel(cfg, *refs):
    width, kinds, ring, d = cfg
    extra = {2: 2, 3: 2}.get(d, 0)
    own_ref, other_ref, gain_ref, w_ref, bias_ref = refs[:5]
    before = refs[5 : 5 + extra]
    rest = refs[5 + extra :]
    pad_ref, raw_ref, lhs_ref = rest[-3:]
    rest = rest[:-3]
    part_ref = rest[0]
    mid_ref = {2: rest[-1], 3: rest[0]}.get(d)
    if d == 3:
        mid_ref, part_ref = rest
    tile, chan_id, tiles = lax.axis_index("tile"), lax.axis_index("chan"), lax.axis_size("tile")
    seq, seqs = lax.axis_index("seq"), lax.axis_size("seq")
    chan = gain_ref.shape[1] // 2
    out_rows = (width - 2) * PITCH
    gain = gain_ref[...]
    pad_ref[...] = jnp.zeros_like(pad_ref)
    raw_ref[...] = jnp.zeros_like(raw_ref)
    main = width * ROWS_DEV

    def place(raw, act, top):
        first = HEAD - 2 if top else HEAD + ROWS_DEV
        for w in range(width):
            pad_ref[w * PITCH + first : w * PITCH + first + 2, :] = act[2 * w : 2 * w + 2]
            raw_ref[w * PITCH + first : w * PITCH + first + 2, :] = raw[2 * w : 2 * w + 2]

    fields = []
    for p in range(2):
        mine = own_ref[:, p * chan : (p + 1) * chan]
        theirs = other_ref[:, p * chan : (p + 1) * chan]
        low = jnp.where(chan_id == 0, mine, theirs)
        high = jnp.where(chan_id == 0, theirs, mine)
        x = jnp.concatenate([low, high], axis=1).astype(f32)
        scale = lax.rsqrt(jnp.mean(x * x, axis=-1, keepdims=True) + norm_eps)
        v = x * scale * gain
        act = v / (1.0 + jnp.exp(-v))
        raw = mine.astype(f32)
        for w in range(width):
            to = slice(w * PITCH + HEAD, w * PITCH + HEAD + ROWS_DEV)
            pad_ref[to, :] = act[w * ROWS_DEV : (w + 1) * ROWS_DEV]
            raw_ref[to, :] = raw[w * ROWS_DEV : (w + 1) * ROWS_DEV]
        for k, kind in enumerate(kinds):
            at = main + k * border_rows(width)
            raw_k, act_k = raw[at : at + 2 * width], act[at : at + 2 * width]
            if kind in ("top", "bottom"):
                place(raw_k, act_k, kind == "top")
            else:
                below = lax.rem(tile + int(kind), 2) == 0
                pl.when(below)(functools.partial(place, raw_k, act_k, False))
                pl.when(jnp.logical_not(below))(functools.partial(place, raw_k, act_k, True))
        for dh in range(3):
            shifted = pad_ref[HEAD - 2 + dh : HEAD - 2 + dh + width * PITCH, :]
            lhs_ref[p, :, dh * 2 * chan : (dh + 1) * 2 * chan] = shifted.astype(bf16)
        part_ref[p] = raw_ref[PITCH + HEAD - 1 : PITCH + HEAD - 1 + out_rows, :]

    lhs = jnp.concatenate(
        [lhs_ref[:, dw * PITCH : dw * PITCH + out_rows, :].reshape(2 * out_rows, 6 * chan) for dw in range(3)], axis=1
    )
    zero = jnp.zeros((out_rows, chan), f32)
    for dt in (2, 1, 0):
        taps = [w_ref[dt * 9 + dh * 3 + dw] for dw in range(3) for dh in range(3)]
        total = dot_nt(lhs, jnp.concatenate(taps, axis=1)).reshape(2, out_rows, chan)
        if dt == 2:
            part_ref[0] += total[0]
            part_ref[1] += total[1]
        elif dt == 1:
            part_ref[1] += total[0]
            part_ref[2] = total[1]
        else:
            part_ref[2] += total[0]
            part_ref[3] = total[1]

    if d >= 2:
        r = lax.broadcasted_iota(jnp.int32, (out_rows, 1), 0)
        h = jnp.bitwise_and(r, PITCH - 1) - 1
        good = (h >= jnp.where(tile == 0, 0, -1)) & (h < jnp.where(tile == tiles - 1, ROWS_DEV, ROWS_DEV + 1))
        good = good & (r >= jnp.where(seq == 0, PITCH, 0)) & (r < jnp.where(seq == seqs - 1, out_rows - PITCH, out_rows))
        base = seq if ring else 0
        if d == 2:
            sums = [(0, before[0], before[1]), (1, before[1], part_ref)]
        else:
            sums = [(2, before[1], part_ref), (3, part_ref, before[0])]
        for k, (shift, now, past) in enumerate(sums):
            first = lax.rem(base - shift + PAIRS, PAIRS) == 0
            mids = []
            for p in range(2):
                value = now[p] + jnp.where(first, 0.0, past[2 + p]) + bias_ref[...]
                mids.append(jnp.where(good, value, 0.0))
            mid_ref[k] = jnp.concatenate(mids, axis=1).astype(bf16)


def tap_kernel(w_ref, out_ref, rows_ref):
    out_chan, chans = w_ref.shape[1:]
    rows_ref[...] = jnp.zeros_like(rows_ref)
    taps = [[w_ref[dr * 3 + ds].astype(f32) for ds in range(3)] for dr in range(3)]
    by_row = [[[taps[0][s] for s in range(3)], [taps[1][s] + taps[2][s] for s in range(3)]]]
    by_row.append([[taps[0][s] + taps[1][s] for s in range(3)], [taps[2][s] for s in range(3)]])
    for i in range(2):
        for dw in range(3):
            for a in range(2):
                t = by_row[i][a]
                zero = jnp.zeros_like(t[0])
                left = (t[0], t[1] + t[2], zero)[dw]
                right = (zero, t[0] + t[1], t[2])[dw]
                for k in range(chans // 128):
                    lanes = slice(k * 128, (k + 1) * 128)
                    rows_ref[pl.ds(0, out_chan, stride=2), :] = left[:, lanes]
                    rows_ref[pl.ds(1, out_chan, stride=2), :] = right[:, lanes]
                    to = a * chans + k * 128
                    out_ref[i, dw, :, to : to + 128] = rows_ref[...].astype(bf16)


def up_kernel(cfg, *refs):
    mid_w, ring, first = cfg
    own_ref, other_ref, w_ref, bias_ref = refs[:4]
    out_ref, lhs_ref, rows_ref, held_ref, sems = refs[-5:]
    chan_id = lax.axis_index("chan")
    base = lax.axis_index("seq") if ring else 0
    chan = own_ref.shape[2] // 2
    cols = mid_w - 2
    keep = (mid_w - 1) * PITCH + ROWS_DEV
    count = own_ref.shape[0]
    frames = 2 * count
    lanes = w_ref.shape[2]
    span = cols * PITCH
    lhs_ref[:, keep:, :] = jnp.zeros_like(lhs_ref[:, keep:, :])
    for k in range(count):
        for p in range(2):
            mine = own_ref[k, :, p * chan : (p + 1) * chan]
            theirs = other_ref[k, :, p * chan : (p + 1) * chan]
            low = jnp.where(chan_id == 0, mine, theirs)
            high = jnp.where(chan_id == 0, theirs, mine)
            x = jnp.concatenate([low, high], axis=1).astype(f32)
            for a in range(3):
                lhs_ref[2 * k + p, 0:keep, a * 2 * chan : (a + 1) * 2 * chan] = x[a : a + keep].astype(bf16)
    for i in range(2):
        lhs = jnp.concatenate(
            [
                lhs_ref[:, dw * PITCH : dw * PITCH + span, i * 2 * chan : (i + 2) * 2 * chan].reshape(frames * span, 4 * chan)
                for dw in range(3)
            ],
            axis=1,
        )
        total = dot_nt(lhs, jnp.concatenate([w_ref[i, dw] for dw in range(3)], axis=1))
        total = total.reshape(frames, span, lanes)
        for f in range(frames):
            for w in range(cols):
                for k in range(lanes // 128):
                    piece = total[f, w * PITCH : w * PITCH + ROWS_DEV, k * 128 : (k + 1) * 128]
                    rows_ref[k, f * cols + w, pl.ds(i, ROWS_DEV, stride=2), :] = piece
    bias = bias_ref[...]
    copies = []
    for k in range(count):
        for f in (2 * k, 2 * k + 1):
            for w in range(cols):
                row = jnp.concatenate([rows_ref[c, f * cols + w] for c in range(lanes // 128)], axis=1)
                held_ref[f, w] = (row[:, : held_ref.shape[3]] + bias).astype(bf16)
        frame = 2 * lax.rem(base - (first + k) + PAIRS, PAIRS)
        copies.append(pltpu.make_async_copy(held_ref.at[pl.ds(2 * k, 2)], out_ref.at[pl.ds(frame, 2)], sems.at[k]))
        copies[-1].start()
    for copy in copies:
        copy.wait()


def swap_chan(x):
    return lax.ppermute(x, "chan", [(0, 1), (1, 0)])


def tile_pairs(color, tiles):
    out = []
    for t in range(color, tiles - 1, 2):
        out += [(t, t + 1), (t + 1, t)]
    return out


def arrive_by_ring(latents, cols):
    seqs, tiles = lax.axis_size("seq"), lax.axis_size("tile")
    colors = min(2, tiles - 1)
    width, span = cols + 4, cols * seqs
    chan = latents.shape[2]
    x = latents[0].T
    edge = jax.ShapeDtypeStruct((chan, 2 * round_up(2 * span, 64)), bf16)
    edges = call(functools.partial(edge_kernel, span, colors), [edge] * colors, [VM], [VM] * colors, [], 4, "edge")(x)
    edges = [lax.ppermute(e, "tile", tile_pairs(color, tiles)) for color, e in enumerate(edges)]
    border = border_rows(width)
    rows = width * ROWS_DEV + colors * border
    block = jax.ShapeDtypeStruct((rows, 2 * chan), bf16)
    windows = call(functools.partial(pack_kernel, seqs, cols), [block] * seqs, [VM], [VM] * seqs, [], 12, "pack", flops=2 * 10**9)(x)
    windows = call(
        functools.partial(border_kernel, seqs, cols, colors),
        [block] * seqs,
        [VM] * colors + [ANY] * seqs,
        [ANY] * seqs,
        [pltpu.VMEM((seqs, colors * border, 2 * chan), bf16), pltpu.SemaphoreType.DMA((seqs,))],
        4,
        "border",
        aliases={colors + d: d for d in range(seqs)},
    )(*edges, *windows)
    blocks = [windows[0]]
    for d in range(1, seqs):
        blocks.append(lax.ppermute(windows[d], "seq", [(i, (i + d) % seqs) for i in range(seqs)]))
    return blocks, [str(c) for c in range(colors)]


def extended(cells, sides, width):
    for axis, dim in sides:
        count = lax.axis_size(axis)
        ends = count - 1
        head = lax.slice_in_dim(cells, 0, width, axis=dim)
        tail = lax.slice_in_dim(cells, cells.shape[dim] - width, cells.shape[dim], axis=dim)
        cells = jnp.concatenate(
            [
                lax.ppermute(tail, axis, [(i, (i + 1) % count) for i in range(ends)]),
                cells,
                lax.ppermute(head, axis, [((i + 1) % count, i) for i in range(ends)]),
            ],
            axis=dim,
        )
    return cells


def arrive_by_all_to_all(latents, cols):
    seqs = lax.axis_size("seq")
    chan = latents.shape[2]
    width = cols + 4
    arranged = latents[0].reshape(FRAMES * ROWS_DEV // seqs, seqs, cols, chan)
    regrouped = lax.all_to_all(arranged, "seq", split_axis=1, concat_axis=0, tiled=True)
    field = regrouped.reshape(FRAMES, ROWS_DEV, cols, chan)
    field = extended(field, (("seq", 2), ("tile", 1)), 2)
    paired = field.reshape(PAIRS, 2, ROWS_DEV + 4, width, chan).transpose(0, 3, 2, 1, 4)
    paired = paired.reshape(PAIRS, width, ROWS_DEV + 4, 2 * chan)
    spare = ((0, border_rows(width) - 2 * width), (0, 0))
    blocks = []
    for d in range(PAIRS):
        k = -d % PAIRS
        pieces = [paired[k, :, 2:-2].reshape(-1, 2 * chan)]
        pieces += [jnp.pad(b.reshape(-1, 2 * chan), spare) for b in (paired[k, :, :2], paired[k, :, -2:])]
        blocks.append(jnp.concatenate(pieces, axis=0))
    return blocks, ["top", "bottom"]


def body(latents, norm_gain, conv_weight, conv_bias, upsample_weight, upsample_bias):
    chan, out_chan = conv_bias.shape[0], upsample_bias.shape[0]
    cols = latents.shape[1] // (FRAMES * ROWS_DEV)
    width, mid_w = cols + 4, cols + 2
    out_rows = mid_w * PITCH
    ring = 2 * lax.axis_size("seq") == FRAMES
    blocks, kinds = arrive_by_ring(latents, cols) if ring else arrive_by_all_to_all(latents, cols)

    up_lanes = round_up(2 * out_chan, 128)
    taps = upsample_weight.transpose(0, 1, 3, 2).reshape(9, out_chan, 2 * chan)
    up_weights = call(
        tap_kernel,
        jax.ShapeDtypeStruct((2, 3, up_lanes, 4 * chan), bf16),
        [VM],
        VM,
        [pltpu.VMEM((up_lanes, 128), f32)],
        12,
        "taps",
        flops=10**9,
    )(taps)
    up_bias = jnp.repeat(upsample_bias, 2)[None]

    weights = conv_weight.transpose(0, 1, 2, 4, 3).reshape(27, chan, 2 * chan)
    gain, bias = norm_gain[None], conv_bias[None]
    part = jax.ShapeDtypeStruct((4, out_rows, chan), f32)
    mid = jax.ShapeDtypeStruct((2, out_rows, 2 * chan), bf16)
    work = [
        pltpu.VMEM((width * PITCH + 2 * HEAD, 2 * chan), f32),
        pltpu.VMEM((width * PITCH + 2 * HEAD, chan), f32),
        pltpu.VMEM((2, width * PITCH, 6 * chan), bf16),
    ]

    def conv(d, out_shape, *before, scratch=()):
        return call(
            functools.partial(conv_kernel, (width, kinds, ring, d)),
            out_shape,
            [VM] * (5 + len(before)),
            [VM] * len(out_shape),
            [*scratch, *work],
            14,
            f"conv{d}",
            flops=2 * 2 * out_rows * 27 * 2 * chan * 256,
        )(blocks[d], swap_chan(blocks[d]), gain, weights, bias, *before)

    def upsample(mids, first, out=None):
        held = () if out is None else (out,)
        return call(
            functools.partial(up_kernel, (mid_w, ring, first)),
            jax.ShapeDtypeStruct((FRAMES, cols, 2 * ROWS_DEV, 2 * out_chan), bf16),
            [VM] * 4 + [ANY] * len(held),
            ANY,
            [
                pltpu.VMEM((4, out_rows, 6 * chan), bf16),
                pltpu.VMEM((up_lanes // 128, 4 * cols, 2 * ROWS_DEV, 128), f32),
                pltpu.VMEM((4, cols, 2 * ROWS_DEV, 2 * out_chan), bf16),
                pltpu.SemaphoreType.DMA((2,)),
            ],
            14,
            f"up{first}",
            flops=2 * 2 * 4 * cols * PITCH * 12 * chan * 256,
            aliases={4: 0} if held else None,
        )(mids, swap_chan(mids), up_weights, up_bias, *held)

    (part0,) = conv(0, [part])
    (part1,) = conv(1, [part])
    part2, early = conv(2, [part, mid], part0, part1)
    decoded = upsample(early, 0)
    (late,) = conv(3, [mid], part0, part2, scratch=[pltpu.VMEM((4, out_rows, chan), f32)])
    decoded = upsample(late, 2, decoded)
    return decoded.transpose(0, 2, 1, 3)


def solution(mesh):
    in_specs = (
        P("tile", ("groups", "seq"), "chan"),
        P(),
        P(None, None, None, None, "chan"),
        P("chan"),
        P(None, None, None, "chan"),
        P("chan"),
    )
    out_specs = P(None, ("groups", "tile"), "seq", "chan")
    return jax.shard_map(body, mesh=mesh, in_specs=in_specs, out_specs=out_specs, check_vma=False)
```

time: 154 us -> 49.1 us (0.32)
  matrix products: 37.8 us -> 0 us
  blocking collectives: 28.2 us -> 0 us
  Pallas kernels: 0 us -> 23 us
  waiting for transfers between devices: 35 us -> 14.1 us
  local copies, waits for them, and re-layouts: 21.3 us -> 2.23 us
  between operations: 13.6 us -> 0.3 us
  starting transfers between devices: 14.8 us -> 9.36 us
  other arithmetic: 3.28 us -> 0 us
    conv_general_dilated x2 -> x0, matrix products: 37.8 us -> none  [the longest x1 29.8 us: body(): lax.conv_general_dilated(shifted[None], conv_weight, (1, 1, 1), 'VALID',...]
    all_to_all x1 -> x0, blocking collectives: 25.4 us -> none  [body(): lax.all_to_all(arranged, 'seq', split_axis=1, concat_axis=0, tiled=True)]
    pallas_call x0 -> x10, Pallas kernels: none -> 23 us  [the longest x4 14.5 us: conv(): call(functools.partial(conv_kernel, (width, kinds, ring, d)), out_shape,...]
    all_gather x1 -> x0, waiting for transfers between devices: 14.2 us -> none  [body(): middle_full = lax.all_gather(middle_rim, 'chan', axis=3, tiled=True)]
    all_gather x2 -> x0, local copies, waits for them, and re-layouts: 10.3 us -> none  [the longest x1 9.9 us: body(): middle_full = lax.all_gather(middle_rim, 'chan', axis=3, tiled=True)]
    ppermute x8 -> x10, waiting for transfers between devices: 20.8 us -> 14.1 us  [the longest x3 13.8 us: arrive_by_ring(): lax.ppermute(windows[d], 'seq', [(i, (i + d) % seqs) for i in range(seqs)])]
    ppermute x8 -> x10, starting transfers between devices: 14.8 us -> 9.36 us  [the longest x3 5.2 us: arrive_by_ring(): lax.ppermute(windows[d], 'seq', [(i, (i + d) % seqs) for i in range(seqs)])]
    convert_element_type x2 -> x0, local copies, waits for them, and re-layouts: 5.44 us -> none  [body(): return image.astype(jnp.bfloat16)]
  transfers between devices with their start and end apart: 9 -> 10, of which waited for: 9 -> 3; matrix products, arithmetic and copies ran while one was open for 0% -> 0% of each run, Pallas kernels for 0% -> 38%
where the time goes in v1:
time: 49.1 us; the launch traced here: 49 us
  Pallas kernels  23 us (47%)
  waiting for transfers between devices  14.1 us (29%)
  starting transfers between devices  9.36 us (19%)
  local copies, waits for them, and re-layouts  2.23 us (5%)
    pallas_call x4, Pallas kernels, conv(): call(functools.partial(conv_kernel, (width, kinds, ring, d)), out_shape,...  14.5 us
    ppermute x3, waiting for transfers between devices, arrive_by_ring(): lax.ppermute(windows[d], 'seq', [(i, (i + d) % seqs) for i in range(seqs)])  13.8 us
    pallas_call x2, Pallas kernels, upsample(): call(functools.partial(up_kernel, (mid_w, ring, first)), jax.ShapeDtypeSt...  5.44 us
    ppermute x3, starting transfers between devices, arrive_by_ring(): lax.ppermute(windows[d], 'seq', [(i, (i + d) % seqs) for i in range(seqs)])  5.2 us
    ppermute x1, starting transfers between devices, arrive_by_ring(): lax.ppermute(e, 'tile', tile_pairs(color, tiles))  3.03 us
    unnamed x14, local copies, waits for them, and re-layouts  2.01 us
    pallas_call x1, Pallas kernels, arrive_by_ring(): call(functools.partial(border_kernel, seqs, cols, colors), [block] * seqs...  1.29 us
    ppermute x6, starting transfers between devices, swap_chan(): return lax.ppermute(x, 'chan', [(0, 1), (1, 0)])  1.13 us
  transfers between devices with their start and end apart: 10, of which 3 were waited for; matrix products, arithmetic and copies ran while one was open for 0% of the time, Pallas kernels for 38%

profile of v1, /device:TPU:0, one launch (start us, length us, event | category | flops | bytes accessed | tf_op | source)
XLA Modules:
  0.0 49.0 jit_solution(17082587839903349535)
XLA Ops:
  0.0 1.0 %copy-done = bf16[1,960,192]{1,2,0:T(8,128)(2,1)S(1)} copy-done((bf16[1,960,192]{1,2,0:T(8,128)(2,1)S(1)}, bf16[1,960,192]{1,2,0:T(8,128)(2,1)}, u32[]{:S(2)}) %copy-start) | copy-done | bytes 368664
  1.0 0.2 edge.1
  1.2 3.0 %collective-permute-start = (bf16[192,128]{1,0:T(8,128)(2,1)S(1)}, bf16[192,128]{1,0:T(8,128)(2,1)S(1)}, u32[]{:S(2)}, u32[]{:S(2)}) collective-permute-start(bf16[192,128]{1,0:T(8,128)(2,1)S(1)} %edge.1), channel_id=1, source_target_pairs={{0,2},{2,0},{1,3},{3,1},{4,6},{6,4},{5,7},{7,5},{8,10},{10,8},{9,1... | collective-permute-start | bytes 147464 | tf_op jit(solution)/shard_map/ppermute | solution.py:297
  4.2 1.0 %copy-done.1 = bf16[1,960,192]{1,2,0:T(8,128)(2,1)S(1)} copy-done((bf16[1,960,192]{1,2,0:T(8,128)(2,1)S(1)}, bf16[1,960,192]{1,2,0:T(8,128)(2,1)}, u32[]{:S(2)}) %copy-start.1) | copy-done | bytes 368664
  5.2 0.8 %pack.1 = (bf16[240,384]{1,0:T(8,128)(2,1)S(1)}, bf16[240,384]{1,0:T(8,128)(2,1)S(1)}, bf16[240,384]{1,0:T(8,128)(2,1)S(1)}, bf16[240,384]{1,0:T(8,128)(2,1)S(1)}) custom-call(bf16[192,960]{1,0:T(8,128)(2,1)S(1)} %bitcast.12), custom_call_target="tpu_custom_call" | custom-call | flops 2000000000 | tf_op jit(solution)/shard_map/pack/pallas_call | solution.py:301
  6.0 0.3 collective-permute-done.refs_0_
  6.3 1.3 %border.1 = (bf16[240,384]{1,0:T(8,128)(2,1)S(1)}, bf16[240,384]{1,0:T(8,128)(2,1)S(1)}, bf16[240,384]{1,0:T(8,128)(2,1)S(1)}, bf16[240,384]{1,0:T(8,128)(2,1)S(1)}) custom-call(bf16[192,128]{1,0:T(8,128)(2,1)S(1)} %collective-permute-done.refs_0_, ...), custom_call_target="tpu_custom_call", output_to_operand_aliasing={{0}: (1, {}), {1}: (2, {}), {2}: (3, {}), {3}: (4, {})} | custom-call | tf_op jit(solution)/shard_map/border/pallas_call | solution.py:302
  7.6 4.2 %collective-permute-start.1 = (bf16[240,384]{1,0:T(8,128)(2,1)S(1)}, bf16[240,384]{1,0:T(8,128)(2,1)S(1)}, u32[]{:S(2)}, u32[]{:S(2)}) collective-permute-start(bf16[240,384]{1,0:T(8,128)(2,1)S(1)} %get-tuple-element.19), channel_id=1, source_target_pairs={{0,12},{4,0},{8,4},{12,8},{1,13},{5,1},{9,5},{13,9},{2,14},{6,2},{... | collective-permute-start | bytes 552968 | tf_op jit(solution)/shard_map/ppermute | solution.py:314
  11.8 1.0 %collective-permute-start.6 = (bf16[240,384]{1,0:T(8,128)(2,1)S(1)}, bf16[240,384]{1,0:T(8,128)(2,1)S(1)}, u32[]{:S(2)}, u32[]{:S(2)}) collective-permute-start(bf16[240,384]{1,0:T(8,128)(2,1)S(1)} %get-tuple-element.22), channel_id=1, source_target_pairs={{0,4},{4,8},{8,12},{12,0},{1,5},{5,9},{9,13},{13,1},{2,6},{6,10},{... | collective-permute-start | bytes 552968 | tf_op jit(solution)/shard_map/ppermute | solution.py:314
  12.8 0.0 collective-permute-start.3
  12.8 4.0 %collective-permute-done.1.refs_0_ = bf16[240,384]{1,0:T(8,128)(2,1)S(1)} collective-permute-done((bf16[240,384]{1,0:T(8,128)(2,1)S(1)}, bf16[240,384]{1,0:T(8,128)(2,1)S(1)}, u32[]{:S(2)}, u32[]{:S(2)}) %collective-permute-start.1) | collective-permute-done | bytes 184352 | tf_op jit(solution)/shard_map/ppermute | solution.py:314
  16.9 9.7 %collective-permute-done.4.refs_0_ = bf16[240,384]{1,0:T(8,128)(2,1)S(1)} collective-permute-done((bf16[240,384]{1,0:T(8,128)(2,1)S(1)}, bf16[240,384]{1,0:T(8,128)(2,1)S(1)}, u32[]{:S(2)}, u32[]{:S(2)}) %collective-permute-start.4) | collective-permute-done | bytes 184352 | tf_op jit(solution)/shard_map/ppermute | solution.py:314
  26.6 0.0 collective-permute-start.5
  26.6 0.0 collective-permute-done.6.refs_0_
  26.6 0.5 %collective-permute-start.7 = (bf16[240,384]{1,0:T(8,128)(2,1)S(1)}, bf16[240,384]{1,0:T(8,128)(2,1)S(1)}, u32[]{:S(2)}, u32[]{:S(2)}) collective-permute-start(bf16[240,384]{1,0:T(8,128)(2,1)S(1)} %collective-permute-done.6.refs_0_), channel_id=1, source_target_pairs={{0,1},{1,0},{2,3},{3,2},{4,5},{5,4},{6,7},{7,6},{8,9},{9,8},{10,11... | collective-permute-start | bytes 552968 | tf_op jit(solution)/shard_map/ppermute | solution.py:279
  27.1 0.0 collective-permute-done.3.refs_1_
  27.1 3.5 %conv0.1.refs_5_ = f32[4,224,192]{2,1,0:T(8,128)S(1)} custom-call(bf16[240,384]{1,0:T(8,128)(2,1)S(1)} %get-tuple-element.20.refs_0_, bf16[240,384]{1,0:T(8,128)(2,1)S(1)} %collective-permute-done.3.refs_1_, f32[1,384]{1,0:T(1,128)S(1)} %broadcast_in_dim.9.refs_2_, bf16[27,192,384]{2,1,0:T(8,128)(2,1)S(1)} %bitcast.13, f32[1,192]{1,0:T(1,128)S(1)} %bitcast.18), custom_call_target="tpu_custom_call" | custom-call | flops 2378170368 | tf_op jit(solution)/shard_map/conv0/pallas_call | solution.py:388
  30.6 0.0 collective-permute-done.7.refs_1_
  30.7 3.5 %conv1.1.refs_6_ = f32[4,224,192]{2,1,0:T(8,128)S(1)} custom-call(bf16[240,384]{1,0:T(8,128)(2,1)S(1)} %collective-permute-done.6.refs_0_, bf16[240,384]{1,0:T(8,128)(2,1)S(1)} %collective-permute-done.7.refs_1_, f32[1,384]{1,0:T(1,128)S(1)} %broadcast_in_dim.9.refs_2_, bf16[27,192,384]{2,1,0:T(8,128)(2,1)S(1)} %bitcast.14, f32[1,192]{1,0:T(1,128)S(1)} %bitcast.19), custom_call_target="tpu_custom_call" | custom-call | flops 2378170368 | tf_op jit(solution)/shard_map/conv1/pallas_call | solution.py:388
  34.2 0.0 collective-permute-done.5.refs_1_
  34.2 3.6 %conv2.1 = (f32[4,224,192]{2,1,0:T(8,128)S(1)}, bf16[2,224,384]{2,1,0:T(8,128)(2,1)S(1)}) custom-call(bf16[240,384]{1,0:T(8,128)(2,1)S(1)} %collective-permute-done.4.refs_0_, bf16[240,384]{1,0:T(8,128)(2,1)S(1)} %collective-permute-done.5.refs_1_, f32[1,384]{1,0:T(1,128)S(1)} %broadcast_in_dim.9.refs_2_, bf16[27,192,384]{2,1,0:T(8,128)(2,1)S(1)} %bitcast.15, ...), custom_call_target="tpu_custom_call" | custom-call | flops 2378170368 | tf_op jit(solution)/shard_map/conv2/pallas_call | solution.py:388
  37.8 0.1 collective-permute-start.9
  37.9 0.0 copy-start.6
  37.9 0.0 copy-start.3
  37.9 3.8 %conv3.1.refs_0_ = bf16[2,224,384]{2,1,0:T(8,128)(2,1)S(1)} custom-call(bf16[240,384]{1,0:T(8,128)(2,1)S(1)} %collective-permute-done.1.refs_0_, bf16[240,384]{1,0:T(8,128)(2,1)S(1)} %collective-permute-done.2.refs_1_, f32[1,384]{1,0:T(1,128)S(1)} %broadcast_in_dim.9.refs_2_, bf16[27,192,384]{2,1,0:T(8,128)(2,1)S(1)} %bitcast.16, f32[1,192]{1,0:T(1,128)S(1)} %bitcast.21, ...), custom_call_target="tpu_custom_call" | custom-call | flops 2378170368 | tf_op jit(solution)/shard_map/conv3/pallas_call | solution.py:388
  41.7 0.5 %collective-permute-start.8 = (bf16[2,224,384]{2,1,0:T(8,128)(2,1)S(1)}, bf16[2,224,384]{2,1,0:T(8,128)(2,1)S(1)}, u32[]{:S(2)}, u32[]{:S(2)}) collective-permute-start(bf16[2,224,384]{2,1,0:T(8,128)(2,1)S(1)} %conv3.1.refs_0_), channel_id=1, source_target_pairs={{0,1},{1,0},{2,3},{3,2},{4,5},{5,4},{6,7},{7,6},{8,9},{9,8},{10,11... | collective-permute-start | bytes 1032200 | tf_op jit(solution)/shard_map/ppermute | solution.py:279
  42.3 0.1 broadcast_in_dim.11
  42.4 0.1 broadcast_in_dim_reshape.3.refs_3_
  42.5 0.8 %taps.1.refs_2_ = bf16[2,3,256,768]{3,2,1,0:T(8,128)(2,1)S(1)} custom-call(bf16[9,96,384]{2,1,0:T(8,128)(2,1)S(1)} %bitcast.17), custom_call_target="tpu_custom_call" | custom-call | flops 1000000000 | tf_op jit(solution)/shard_map/taps/pallas_call | solution.py:365
  43.3 0.0 collective-permute-done.9.refs_1_
  43.3 2.7 %up0.1.refs_4_ = bf16[8,5,48,192]{3,2,1,0:T(8,128)(2,1)} custom-call(bf16[2,224,384]{2,1,0:T(8,128)(2,1)S(1)} %get-tuple-element.24.refs_0_, bf16[2,224,384]{2,1,0:T(8,128)(2,1)S(1)} %collective-permute-done.9.refs_1_, bf16[2,3,256,768]{3,2,1,0:T(8,128)(2,1)S(1)} %taps.1.refs_2_, f32[1,192]{1,0:T(1,128)S(1)} %broadcast_in_dim_reshape.3.refs_3_), custom_call_target="tpu_custom_call" | custom-call | flops 1509949440 | tf_op jit(solution)/shard_map/up0/pallas_call | solution.py:401
  46.1 2.7 %up2.1 = bf16[8,5,48,192]{3,2,1,0:T(8,128)(2,1)} custom-call(bf16[2,224,384]{2,1,0:T(8,128)(2,1)S(1)} %conv3.1.refs_0_, bf16[2,224,384]{2,1,0:T(8,128)(2,1)S(1)} %collective-permute-done.8.refs_1_, bf16[2,3,256,768]{3,2,1,0:T(8,128)(2,1)S(1)} %taps.1.refs_2_, f32[1,192]{1,0:T(1,128)S(1)} %broadcast_in_dim_reshape.3.refs_3_, ...), custom_call_target="tpu_custom_call", output_to_operand_aliasing={{}: (4, {})} | custom-call | flops 1509949440 | tf_op jit(solution)/shard_map/up2/pallas_call | solution.py:401
  (15 shorter events, 0.0 us)
Async XLA Ops:
  0.0 1.0 %copy-start = (bf16[1,960,192]{1,2,0:T(8,128)(2,1)S(1)}, bf16[1,960,192]{1,2,0:T(8,128)(2,1)}, u32[]{:S(2)}) copy-start(bf16[1,960,192]{1,2,0:T(8,128)(2,1)} %param.6) | copy-start | bytes 1105924
  1.2 5.1 %collective-permute-start = (bf16[192,128]{1,0:T(8,128)(2,1)S(1)}, bf16[192,128]{1,0:T(8,128)(2,1)S(1)}, u32[]{:S(2)}, u32[]{:S(2)}) collective-permute-start(bf16[192,128]{1,0:T(8,128)(2,1)S(1)} %edge.1), channel_id=1, source_target_pairs={{0,2},{2,0},{1,3},{3,1},{4,6},{6,4},{5,7},{7,5},{8,10},{10,8},{9,1... | collective-permute-start | bytes 147464 | tf_op jit(solution)/shard_map/ppermute | solution.py:297
  4.2 1.0 %copy-start.1 = (bf16[1,960,192]{1,2,0:T(8,128)(2,1)S(1)}, bf16[1,960,192]{1,2,0:T(8,128)(2,1)}, u32[]{:S(2)}) copy-start(bf16[1,960,192]{1,2,0:T(8,128)(2,1)} %param.6) | copy-start | bytes 1105924
  5.2 7.6 %copy-start.5 = (f32[384]{0:T(512)S(1)}, f32[384]{0:T(512)}, u32[]{:S(2)}) copy-start(f32[384]{0:T(512)} %param.7) | copy-start | bytes 4612
  5.2 21.9 %copy-start.2 = (bf16[3,3,3,384,192]{3,4,2,1,0:T(8,128)(2,1)S(1)}, bf16[3,3,3,384,192]{3,4,2,1,0:T(8,128)(2,1)}, u32[]{:S(2)}) copy-start(bf16[3,3,3,384,192]{3,4,2,1,0:T(8,128)(2,1)} %param.8) | copy-start | bytes 11943940
  5.2 21.9 %copy-start.4 = (f32[192]{0:T(256)S(1)}, f32[192]{0:T(256)}, u32[]{:S(2)}) copy-start(f32[192]{0:T(256)} %param.9) | copy-start | bytes 2308
  7.6 9.2 %collective-permute-start.1 = (bf16[240,384]{1,0:T(8,128)(2,1)S(1)}, bf16[240,384]{1,0:T(8,128)(2,1)S(1)}, u32[]{:S(2)}, u32[]{:S(2)}) collective-permute-start(bf16[240,384]{1,0:T(8,128)(2,1)S(1)} %get-tuple-element.19), channel_id=1, source_target_pairs={{0,12},{4,0},{8,4},{12,8},{1,13},{5,1},{9,5},{13,9},{2,14},{6,2},{... | collective-permute-start | bytes 552968 | tf_op jit(solution)/shard_map/ppermute | solution.py:314
  11.8 14.8 %collective-permute-start.4 = (bf16[240,384]{1,0:T(8,128)(2,1)S(1)}, bf16[240,384]{1,0:T(8,128)(2,1)S(1)}, u32[]{:S(2)}, u32[]{:S(2)}) collective-permute-start(bf16[240,384]{1,0:T(8,128)(2,1)S(1)} %get-tuple-element.21), channel_id=1, source_target_pairs={{0,8},{4,12},{8,0},{12,4},{1,9},{5,13},{9,1},{13,5},{2,10},{6,14},... | collective-permute-start | bytes 552968 | tf_op jit(solution)/shard_map/ppermute | solution.py:314
  11.8 14.8 %collective-permute-start.6 = (bf16[240,384]{1,0:T(8,128)(2,1)S(1)}, bf16[240,384]{1,0:T(8,128)(2,1)S(1)}, u32[]{:S(2)}, u32[]{:S(2)}) collective-permute-start(bf16[240,384]{1,0:T(8,128)(2,1)S(1)} %get-tuple-element.22), channel_id=1, source_target_pairs={{0,4},{4,8},{8,12},{12,0},{1,5},{5,9},{9,13},{13,1},{2,6},{6,10},{... | collective-permute-start | bytes 552968 | tf_op jit(solution)/shard_map/ppermute | solution.py:314
  12.8 14.3 %collective-permute-start.3 = (bf16[240,384]{1,0:T(8,128)(2,1)S(1)}, bf16[240,384]{1,0:T(8,128)(2,1)S(1)}, u32[]{:S(2)}, u32[]{:S(2)}) collective-permute-start(bf16[240,384]{1,0:T(8,128)(2,1)S(1)} %get-tuple-element.20.refs_0_), channel_id=1, source_target_pairs={{0,1},{1,0},{2,3},{3,2},{4,5},{5,4},{6,7},{7,6},{8,9},{9,8},{10,11... | collective-permute-start | bytes 552968 | tf_op jit(solution)/shard_map/ppermute | solution.py:279
  16.8 21.0 %collective-permute-start.2 = (bf16[240,384]{1,0:T(8,128)(2,1)S(1)}, bf16[240,384]{1,0:T(8,128)(2,1)S(1)}, u32[]{:S(2)}, u32[]{:S(2)}) collective-permute-start(bf16[240,384]{1,0:T(8,128)(2,1)S(1)} %collective-permute-done.1.refs_0_), channel_id=1, source_target_pairs={{0,1},{1,0},{2,3},{3,2},{4,5},{5,4},{6,7},{7,6},{8,9},{9,8},{10,11... | collective-permute-start | bytes 552968 | tf_op jit(solution)/shard_map/ppermute | solution.py:279
  26.6 7.6 %collective-permute-start.5 = (bf16[240,384]{1,0:T(8,128)(2,1)S(1)}, bf16[240,384]{1,0:T(8,128)(2,1)S(1)}, u32[]{:S(2)}, u32[]{:S(2)}) collective-permute-start(bf16[240,384]{1,0:T(8,128)(2,1)S(1)} %collective-permute-done.4.refs_0_), channel_id=1, source_target_pairs={{0,1},{1,0},{2,3},{3,2},{4,5},{5,4},{6,7},{7,6},{8,9},{9,8},{10,11... | collective-permute-start | bytes 552968 | tf_op jit(solution)/shard_map/ppermute | solution.py:279
  26.6 4.0 %collective-permute-start.7 = (bf16[240,384]{1,0:T(8,128)(2,1)S(1)}, bf16[240,384]{1,0:T(8,128)(2,1)S(1)}, u32[]{:S(2)}, u32[]{:S(2)}) collective-permute-start(bf16[240,384]{1,0:T(8,128)(2,1)S(1)} %collective-permute-done.6.refs_0_), channel_id=1, source_target_pairs={{0,1},{1,0},{2,3},{3,2},{4,5},{5,4},{6,7},{7,6},{8,9},{9,8},{10,11... | collective-permute-start | bytes 552968 | tf_op jit(solution)/shard_map/ppermute | solution.py:279
  37.8 5.5 %collective-permute-start.9 = (bf16[2,224,384]{2,1,0:T(8,128)(2,1)S(1)}, bf16[2,224,384]{2,1,0:T(8,128)(2,1)S(1)}, u32[]{:S(2)}, u32[]{:S(2)}) collective-permute-start(bf16[2,224,384]{2,1,0:T(8,128)(2,1)S(1)} %get-tuple-element.24.refs_0_), channel_id=1, source_target_pairs={{0,1},{1,0},{2,3},{3,2},{4,5},{5,4},{6,7},{7,6},{8,9},{9,8},{10,11... | collective-permute-start | bytes 1032200 | tf_op jit(solution)/shard_map/ppermute | solution.py:279
  37.9 4.4 %copy-start.6 = (f32[96]{0:T(128)S(1)}, f32[96]{0:T(128)}, u32[]{:S(2)}) copy-start(f32[96]{0:T(128)} %param.11) | copy-start | bytes 1156
  37.9 4.6 %copy-start.3 = (bf16[3,3,384,96]{2,3,1,0:T(8,128)(2,1)S(1)}, bf16[3,3,384,96]{2,3,1,0:T(8,128)(2,1)}, u32[]{:S(2)}) copy-start(bf16[3,3,384,96]{2,3,1,0:T(8,128)(2,1)} %param.10) | copy-start | bytes 1990660
  41.7 4.3 %collective-permute-start.8 = (bf16[2,224,384]{2,1,0:T(8,128)(2,1)S(1)}, bf16[2,224,384]{2,1,0:T(8,128)(2,1)S(1)}, u32[]{:S(2)}, u32[]{:S(2)}) collective-permute-start(bf16[2,224,384]{2,1,0:T(8,128)(2,1)S(1)} %conv3.1.refs_0_), channel_id=1, source_target_pairs={{0,1},{1,0},{2,3},{3,2},{4,5},{5,4},{6,7},{7,6},{8,9},{9,8},{10,11... | collective-permute-start | bytes 1032200 | tf_op jit(solution)/shard_map/ppermute | solution.py:279

commit v2 on v1

--- a/solution.py
+++ b/solution.py
@@ -7,9 +7,11 @@
 from jax.experimental.pallas import tpu as pltpu
 from jax.sharding import PartitionSpec as P
 
+
 FRAMES = 8
 ROWS_DEV = 24
 PAIRS = FRAMES // 2
+ORDER = (0, 1, 3, 2)
 PITCH = 32
 HEAD = 8
 
@@ -25,7 +27,7 @@
     return lax.dot_general(a, b, (((1,), (1,)), ((), ())), preferred_element_type=f32)
 
 
-def call(kernel, out_shape, in_specs, out_specs, scratch, limit, name, flops=0, moved=0, aliases=None):
+def call(kernel, out_shape, in_specs, out_specs, scratch, limit, flops=0, moved=0, aliases=None):
     return pl.pallas_call(
         kernel,
         out_shape=out_shape,
@@ -35,7 +37,6 @@
         compiler_params=pltpu.CompilerParams(vmem_limit_bytes=limit * MIB),
         input_output_aliases=aliases or {},
         cost_estimate=pl.CostEstimate(flops=flops, bytes_accessed=moved, transcendentals=0),
-        name=name,
     )
 
 
@@ -45,21 +46,6 @@
 
 def border_rows(width):
     return round_up(2 * width, 8)
-
-
-def edge_kernel(span, colors, x_ref, *outs):
-    tile = lax.axis_index("tile")
-    half = ROWS_DEV * span
-    seg = round_up(2 * span, 64)
-    chan = x_ref.shape[0]
-    for color in range(colors):
-        below = lax.rem(tile + color, 2) == 0
-        parts = []
-        for p in range(2):
-            last = x_ref[:, (p + 1) * half - 2 * span : (p + 1) * half]
-            first = x_ref[:, p * half : p * half + 2 * span]
-            parts += [jnp.where(below, last, first), jnp.zeros((chan, seg - 2 * span), bf16)]
-        outs[color][...] = jnp.concatenate(parts, axis=1)
 
 
 def selection(rows, per_col, width, cols, span, dest, tokens):
@@ -75,16 +61,25 @@
     return jnp.where(lane == token, 1.0, 0.0).astype(bf16)
 
 
-def pack_kernel(count, cols, x_ref, *outs):
-    seq = lax.axis_index("seq")
+def pack_kernel(count, cols, colors, x_ref, *outs):
+    seq, tile = lax.axis_index("seq"), lax.axis_index("tile")
     width, span = cols + 4, count * cols
     half = ROWS_DEV * span
-    parts = [x_ref[:, p * half : (p + 1) * half] for p in range(2)]
+    seg = round_up(2 * span, 64)
+    chan = x_ref.shape[0]
+    rows = width * ROWS_DEV
+    for color in range(colors):
+        below = lax.rem(tile + color, 2) == 0
+        parts = []
+        for p in range(2):
+            last = x_ref[:, (p + 1) * half - 2 * span : (p + 1) * half]
+            first = x_ref[:, p * half : p * half + 2 * span]
+            parts += [jnp.where(below, last, first), jnp.zeros((chan, seg - 2 * span), bf16)]
+        outs[color][...] = jnp.concatenate(parts, axis=1)
     for d in range(count):
-        dest = lax.rem(seq + d, count)
-        pick = selection(width * ROWS_DEV, ROWS_DEV, width, cols, span, dest, half)
-        both = jnp.concatenate([dot_nt(pick, part) for part in parts], axis=1)
-        outs[d][0 : width * ROWS_DEV, :] = both.astype(bf16)
+        pick = selection(rows, ROWS_DEV, width, cols, span, lax.rem(seq + d, count), half)
+        both = jnp.concatenate([dot_nt(pick, x_ref[:, p * half : (p + 1) * half]) for p in range(2)], axis=1)
+        outs[colors + d][0:rows, :] = both.astype(bf16)
 
 
 def border_kernel(count, cols, colors, *refs):
@@ -95,14 +90,15 @@
     width, span = cols + 4, count * cols
     rows = border_rows(width)
     seg = round_up(2 * span, 64)
+    picks = [selection(rows, 2, width, cols, span, lax.rem(seq + d, count), seg) for d in range(count)]
+    pick = jnp.concatenate(picks, axis=0)
+    for color in range(colors):
+        x = edges[color][...]
+        both = jnp.concatenate([dot_nt(pick, x[:, p * seg : (p + 1) * seg]) for p in range(2)], axis=1)
+        for d in range(count):
+            held[d, color * rows : (color + 1) * rows, :] = both[d * rows : (d + 1) * rows].astype(bf16)
     copies = []
     for d in range(count):
-        dest = lax.rem(seq + d, count)
-        pick = selection(rows, 2, width, cols, span, dest, seg)
-        for color in range(colors):
-            x = edges[color][...]
-            both = jnp.concatenate([dot_nt(pick, x[:, p * seg : (p + 1) * seg]) for p in range(2)], axis=1)
-            held[d, color * rows : (color + 1) * rows, :] = both.astype(bf16)
         to = outs[d].at[pl.ds(width * ROWS_DEV, colors * rows)]
         copies.append(pltpu.make_async_copy(held.at[d], to, sems.at[d]))
         copies[-1].start()
@@ -111,33 +107,30 @@
 
 
 def conv_kernel(cfg, *refs):
-    width, kinds, ring, d = cfg
-    extra = {2: 2, 3: 2}.get(d, 0)
+    width, kinds, ring, d, done = cfg
     own_ref, other_ref, gain_ref, w_ref, bias_ref = refs[:5]
-    before = refs[5 : 5 + extra]
-    rest = refs[5 + extra :]
+    others = sorted({k for now, past in done for k in (now, past)} - {d})
+    parts = dict(zip(others, refs[5:]))
+    rest = refs[5 + len(others) :]
     pad_ref, raw_ref, lhs_ref = rest[-3:]
-    rest = rest[:-3]
-    part_ref = rest[0]
-    mid_ref = {2: rest[-1], 3: rest[0]}.get(d)
-    if d == 3:
-        mid_ref, part_ref = rest
+    mid_ref = rest[0] if done else None
+    part_ref = rest[1] if done else rest[0]
+    parts[d] = part_ref
     tile, chan_id, tiles = lax.axis_index("tile"), lax.axis_index("chan"), lax.axis_size("tile")
     seq, seqs = lax.axis_index("seq"), lax.axis_size("seq")
-    chan = gain_ref.shape[1] // 2
+    chan = gain_ref.shape[0] // 2
     out_rows = (width - 2) * PITCH
-    gain = gain_ref[...]
+    gain = gain_ref[...].reshape(1, 2 * chan)
     pad_ref[...] = jnp.zeros_like(pad_ref)
     raw_ref[...] = jnp.zeros_like(raw_ref)
     main = width * ROWS_DEV
 
-    def place(raw, act, top):
-        first = HEAD - 2 if top else HEAD + ROWS_DEV
+    def place(raw, act, first):
         for w in range(width):
-            pad_ref[w * PITCH + first : w * PITCH + first + 2, :] = act[2 * w : 2 * w + 2]
-            raw_ref[w * PITCH + first : w * PITCH + first + 2, :] = raw[2 * w : 2 * w + 2]
-
-    fields = []
+            to = slice(w * PITCH + first, w * PITCH + first + 2)
+            pad_ref[to, :] = act[2 * w : 2 * w + 2]
+            raw_ref[to, :] = raw[2 * w : 2 * w + 2]
+
     for p in range(2):
         mine = own_ref[:, p * chan : (p + 1) * chan]
         theirs = other_ref[:, p * chan : (p + 1) * chan]
@@ -152,15 +145,21 @@
             to = slice(w * PITCH + HEAD, w * PITCH + HEAD + ROWS_DEV)
             pad_ref[to, :] = act[w * ROWS_DEV : (w + 1) * ROWS_DEV]
             raw_ref[to, :] = raw[w * ROWS_DEV : (w + 1) * ROWS_DEV]
+        tops, bottoms = [], []
         for k, kind in enumerate(kinds):
             at = main + k * border_rows(width)
-            raw_k, act_k = raw[at : at + 2 * width], act[at : at + 2 * width]
-            if kind in ("top", "bottom"):
-                place(raw_k, act_k, kind == "top")
+            pieces = raw[at : at + 2 * width], act[at : at + 2 * width]
+            if kind == "top":
+                tops.append(pieces)
+            elif kind == "bottom":
+                bottoms.append(pieces)
             else:
                 below = lax.rem(tile + int(kind), 2) == 0
-                pl.when(below)(functools.partial(place, raw_k, act_k, False))
-                pl.when(jnp.logical_not(below))(functools.partial(place, raw_k, act_k, True))
+                tops.append([jnp.where(below, 0.0, piece) for piece in pieces])
+                bottoms.append([jnp.where(below, piece, 0.0) for piece in pieces])
+        for found, first in ((tops, HEAD - 2), (bottoms, HEAD + ROWS_DEV)):
+            if found:
+                place(functools.reduce(jnp.add, [f[0] for f in found]), functools.reduce(jnp.add, [f[1] for f in found]), first)
         for dh in range(3):
             shifted = pad_ref[HEAD - 2 + dh : HEAD - 2 + dh + width * PITCH, :]
             lhs_ref[p, :, dh * 2 * chan : (dh + 1) * 2 * chan] = shifted.astype(bf16)
@@ -183,27 +182,28 @@
             part_ref[2] += total[0]
             part_ref[3] = total[1]
 
-    if d >= 2:
+    if done:
         r = lax.broadcasted_iota(jnp.int32, (out_rows, 1), 0)
         h = jnp.bitwise_and(r, PITCH - 1) - 1
         good = (h >= jnp.where(tile == 0, 0, -1)) & (h < jnp.where(tile == tiles - 1, ROWS_DEV, ROWS_DEV + 1))
         good = good & (r >= jnp.where(seq == 0, PITCH, 0)) & (r < jnp.where(seq == seqs - 1, out_rows - PITCH, out_rows))
         base = seq if ring else 0
-        if d == 2:
-            sums = [(0, before[0], before[1]), (1, before[1], part_ref)]
-        else:
-            sums = [(2, before[1], part_ref), (3, part_ref, before[0])]
-        for k, (shift, now, past) in enumerate(sums):
-            first = lax.rem(base - shift + PAIRS, PAIRS) == 0
+        for k, (now, past) in enumerate(done):
+            first = lax.rem(base - now + PAIRS, PAIRS) == 0
             mids = []
             for p in range(2):
-                value = now[p] + jnp.where(first, 0.0, past[2 + p]) + bias_ref[...]
+                value = parts[now][p] + jnp.where(first, 0.0, parts[past][2 + p]) + bias_ref[...]
                 mids.append(jnp.where(good, value, 0.0))
             mid_ref[k] = jnp.concatenate(mids, axis=1).astype(bf16)
 
 
-def tap_kernel(w_ref, out_ref, rows_ref):
+def tap_kernel(w_ref, bias_ref, out_ref, wide_ref, rows_ref):
     out_chan, chans = w_ref.shape[1:]
+    lane = lax.broadcasted_iota(jnp.int32, (out_chan, wide_ref.shape[1]), 1)
+    row = lax.broadcasted_iota(jnp.int32, lane.shape, 0)
+    spread = jnp.where((lane == 2 * row) | (lane == 2 * row + 1), 1.0, 0.0)
+    dims = (((1,), (0,)), ((), ()))
+    wide_ref[...] = lax.dot_general(bias_ref[...], spread, dims, precision=lax.Precision.HIGHEST, preferred_element_type=f32)
     rows_ref[...] = jnp.zeros_like(rows_ref)
     taps = [[w_ref[dr * 3 + ds].astype(f32) for ds in range(3)] for dr in range(3)]
     by_row = [[[taps[0][s] for s in range(3)], [taps[1][s] + taps[2][s] for s in range(3)]]]
@@ -224,7 +224,7 @@
 
 
 def up_kernel(cfg, *refs):
-    mid_w, ring, first = cfg
+    mid_w, ring, shifts = cfg
     own_ref, other_ref, w_ref, bias_ref = refs[:4]
     out_ref, lhs_ref, rows_ref, held_ref, sems = refs[-5:]
     chan_id = lax.axis_index("chan")
@@ -261,14 +261,14 @@
                 for k in range(lanes // 128):
                     piece = total[f, w * PITCH : w * PITCH + ROWS_DEV, k * 128 : (k + 1) * 128]
                     rows_ref[k, f * cols + w, pl.ds(i, ROWS_DEV, stride=2), :] = piece
-    bias = bias_ref[...]
+    bias = bias_ref[:, : held_ref.shape[3]]
     copies = []
     for k in range(count):
         for f in (2 * k, 2 * k + 1):
             for w in range(cols):
                 row = jnp.concatenate([rows_ref[c, f * cols + w] for c in range(lanes // 128)], axis=1)
                 held_ref[f, w] = (row[:, : held_ref.shape[3]] + bias).astype(bf16)
-        frame = 2 * lax.rem(base - (first + k) + PAIRS, PAIRS)
+        frame = 2 * lax.rem(base - shifts[k] + PAIRS, PAIRS)
         copies.append(pltpu.make_async_copy(held_ref.at[pl.ds(2 * k, 2)], out_ref.at[pl.ds(frame, 2)], sems.at[k]))
         copies[-1].start()
     for copy in copies:
@@ -292,13 +292,21 @@
     width, span = cols + 4, cols * seqs
     chan = latents.shape[2]
     x = latents[0].T
-    edge = jax.ShapeDtypeStruct((chan, 2 * round_up(2 * span, 64)), bf16)
-    edges = call(functools.partial(edge_kernel, span, colors), [edge] * colors, [VM], [VM] * colors, [], 4, "edge")(x)
-    edges = [lax.ppermute(e, "tile", tile_pairs(color, tiles)) for color, e in enumerate(edges)]
     border = border_rows(width)
     rows = width * ROWS_DEV + colors * border
+    edge = jax.ShapeDtypeStruct((chan, 2 * round_up(2 * span, 64)), bf16)
     block = jax.ShapeDtypeStruct((rows, 2 * chan), bf16)
-    windows = call(functools.partial(pack_kernel, seqs, cols), [block] * seqs, [VM], [VM] * seqs, [], 12, "pack", flops=2 * 10**9)(x)
+    packed = call(
+        functools.partial(pack_kernel, seqs, cols, colors),
+        [edge] * colors + [block] * seqs,
+        [VM],
+        [VM] * (colors + seqs),
+        [],
+        12,
+        flops=2 * 10**9,
+    )(x)
+    edges, windows = packed[:colors], packed[colors:]
+    edges = [lax.ppermute(e, "tile", tile_pairs(color, tiles)) for color, e in enumerate(edges)]
     windows = call(
         functools.partial(border_kernel, seqs, cols, colors),
         [block] * seqs,
@@ -306,7 +314,6 @@
         [ANY] * seqs,
         [pltpu.VMEM((seqs, colors * border, 2 * chan), bf16), pltpu.SemaphoreType.DMA((seqs,))],
         4,
-        "border",
         aliases={colors + d: d for d in range(seqs)},
     )(*edges, *windows)
     blocks = [windows[0]]
@@ -352,7 +359,7 @@
     return blocks, ["top", "bottom"]
 
 
-def body(latents, norm_gain, conv_weight, conv_bias, upsample_weight, upsample_bias):
+def block_body(latents, norm_gain, conv_weight, conv_bias, upsample_weight, upsample_bias):
     chan, out_chan = conv_bias.shape[0], upsample_bias.shape[0]
     cols = latents.shape[1] // (FRAMES * ROWS_DEV)
     width, mid_w = cols + 4, cols + 2
@@ -362,65 +369,70 @@
 
     up_lanes = round_up(2 * out_chan, 128)
     taps = upsample_weight.transpose(0, 1, 3, 2).reshape(9, out_chan, 2 * chan)
-    up_weights = call(
+    up_weights, up_bias = call(
         tap_kernel,
-        jax.ShapeDtypeStruct((2, 3, up_lanes, 4 * chan), bf16),
-        [VM],
-        VM,
+        [jax.ShapeDtypeStruct((2, 3, up_lanes, 4 * chan), bf16), jax.ShapeDtypeStruct((1, up_lanes), f32)],
+        [VM, VM],
+        [VM, VM],
         [pltpu.VMEM((up_lanes, 128), f32)],
         12,
-        "taps",
         flops=10**9,
-    )(taps)
-    up_bias = jnp.repeat(upsample_bias, 2)[None]
+    )(taps, upsample_bias[None])
 
     weights = conv_weight.transpose(0, 1, 2, 4, 3).reshape(27, chan, 2 * chan)
-    gain, bias = norm_gain[None], conv_bias[None]
+    gain, bias = norm_gain, conv_bias[None]
     part = jax.ShapeDtypeStruct((4, out_rows, chan), f32)
-    mid = jax.ShapeDtypeStruct((2, out_rows, 2 * chan), bf16)
     work = [
         pltpu.VMEM((width * PITCH + 2 * HEAD, 2 * chan), f32),
         pltpu.VMEM((width * PITCH + 2 * HEAD, chan), f32),
         pltpu.VMEM((2, width * PITCH, 6 * chan), bf16),
     ]
 
-    def conv(d, out_shape, *before, scratch=()):
+    def conv(d, parts=None, done=()):
+        keep = d != ORDER[-1]
+        others = sorted({k for pair in done for k in pair} - {d})
+        before = [parts[k] for k in others]
+        outs = [jax.ShapeDtypeStruct((len(done), out_rows, 2 * chan), bf16)] if done else []
+        outs += [part] if keep else []
+        other = swap_chan(blocks[d])
         return call(
-            functools.partial(conv_kernel, (width, kinds, ring, d)),
-            out_shape,
+            functools.partial(conv_kernel, (width, kinds, ring, d, done)),
+            outs,
             [VM] * (5 + len(before)),
-            [VM] * len(out_shape),
-            [*scratch, *work],
+            [VM] * len(outs),
+            ([] if keep else [pltpu.VMEM((4, out_rows, chan), f32)]) + work,
             14,
-            f"conv{d}",
             flops=2 * 2 * out_rows * 27 * 2 * chan * 256,
-        )(blocks[d], swap_chan(blocks[d]), gain, weights, bias, *before)
-
-    def upsample(mids, first, out=None):
+        )(blocks[d], other, gain, weights, bias, *before)
+
+    def upsample(mids, shifts, out=None):
         held = () if out is None else (out,)
+        count = len(shifts)
+        other = swap_chan(mids)
         return call(
-            functools.partial(up_kernel, (mid_w, ring, first)),
+            functools.partial(up_kernel, (mid_w, ring, shifts)),
             jax.ShapeDtypeStruct((FRAMES, cols, 2 * ROWS_DEV, 2 * out_chan), bf16),
             [VM] * 4 + [ANY] * len(held),
             ANY,
             [
-                pltpu.VMEM((4, out_rows, 6 * chan), bf16),
-                pltpu.VMEM((up_lanes // 128, 4 * cols, 2 * ROWS_DEV, 128), f32),
-                pltpu.VMEM((4, cols, 2 * ROWS_DEV, 2 * out_chan), bf16),
-                pltpu.SemaphoreType.DMA((2,)),
+                pltpu.VMEM((2 * count, out_rows, 6 * chan), bf16),
+                pltpu.VMEM((up_lanes // 128, 2 * count * cols, 2 * ROWS_DEV, 128), f32),
+                pltpu.VMEM((2 * count, cols, 2 * ROWS_DEV, 2 * out_chan), bf16),
+                pltpu.SemaphoreType.DMA((count,)),
             ],
             14,
-            f"up{first}",
-            flops=2 * 2 * 4 * cols * PITCH * 12 * chan * 256,
+            flops=2 * 2 * 2 * count * cols * PITCH * 12 * chan * 256,
             aliases={4: 0} if held else None,
-        )(mids, swap_chan(mids), up_weights, up_bias, *held)
-
-    (part0,) = conv(0, [part])
-    (part1,) = conv(1, [part])
-    part2, early = conv(2, [part, mid], part0, part1)
-    decoded = upsample(early, 0)
-    (late,) = conv(3, [mid], part0, part2, scratch=[pltpu.VMEM((4, out_rows, chan), f32)])
-    decoded = upsample(late, 2, decoded)
+        )(mids, other, up_weights, up_bias, *held)
+
+    parts = {}
+    (parts[0],) = conv(0)
+    mid0, parts[1] = conv(1, parts, ((0, 1),))
+    mid3, parts[3] = conv(3, parts, ((3, 0),))
+    decoded = upsample(mid0, (0,))
+    decoded = upsample(mid3, (3,), decoded)
+    (late,) = conv(2, parts, ((1, 2), (2, 3)))
+    decoded = upsample(late, (1, 2), decoded)
     return decoded.transpose(0, 2, 1, 3)
 
 
@@ -434,4 +446,4 @@
         P("chan"),
     )
     out_specs = P(None, ("groups", "tile"), "seq", "chan")
-    return jax.shard_map(body, mesh=mesh, in_specs=in_specs, out_specs=out_specs, check_vma=False)
+    return jax.shard_map(block_body, mesh=mesh, in_specs=in_specs, out_specs=out_specs, check_vma=False)

time: 49.1 us -> 47.2 us (0.961)
  the two profiles are of different devices: /device:TPU:0 before, /device:TPU:23 now
where the time goes in v2:
time: 47.2 us; the launch traced here: 47.1 us
  Pallas kernels  21.8 us (46%)
  waiting for transfers between devices  13.4 us (28%)
  starting transfers between devices  10.7 us (23%)
  local copies, waits for them, and re-layouts  1.02 us (2%)
    pallas_call x4, Pallas kernels, conv(): call(functools.partial(conv_kernel, (width, kinds, ring, d, done)), outs,...  13.2 us
    ppermute x3, waiting for transfers between devices, arrive_by_ring(): lax.ppermute(windows[d], 'seq', [(i, (i + d) % seqs) for i in range(seqs)])  10.6 us
    ppermute x7, starting transfers between devices, swap_chan(): return lax.ppermute(x, 'chan', [(0, 1), (1, 0)])  7.8 us
    pallas_call x3, Pallas kernels, upsample(): call(functools.partial(up_kernel, (mid_w, ring, shifts)), jax.ShapeDtypeS...  6.47 us
    ppermute x1, waiting for transfers between devices, arrive_by_ring(): lax.ppermute(e, 'tile', tile_pairs(color, tiles))  2.69 us
    ppermute x3, starting transfers between devices, arrive_by_ring(): lax.ppermute(windows[d], 'seq', [(i, (i + d) % seqs) for i in range(seqs)])  2.55 us
    unnamed x12, local copies, waits for them, and re-layouts  1.02 us
  transfers between devices with their start and end apart: 11, of which 4 were waited for; matrix products, arithmetic and copies ran while one was open for 0% of the time, Pallas kernels for 31%

profile of v2, /device:TPU:23, one launch (start us, length us, event | category | flops | bytes accessed | tf_op | source)
XLA Modules:
  0.0 47.1 jit_solution(7564900832759678915)
XLA Ops:
  0.0 1.0 %copy-done.2 = bf16[1,960,192]{1,2,0:T(8,128)(2,1)S(1)} copy-done((bf16[1,960,192]{1,2,0:T(8,128)(2,1)S(1)}, bf16[1,960,192]{1,2,0:T(8,128)(2,1)}, u32[]{:S(2)}) %copy-start.2) | copy-done | bytes 368664
  1.0 0.8 %shard_map.64 = (bf16[192,128]{1,0:T(8,128)(2,1)S(1)}, bf16[240,384]{1,0:T(8,128)(2,1)S(1)}, bf16[240,384]{1,0:T(8,128)(2,1)S(1)}, bf16[240,384]{1,0:T(8,128)(2,1)S(1)}, bf16[240,384]{1,0:T(8,128)(2,1)S(1)}) custom-call(bf16[192,960]{1,0:T(8,128)(2,1)S(1)} %bitcast.17), custom_call_target="tpu_custom_call" | custom-call | flops 2000000000 | tf_op jit(solution)/shard_map/pallas_call | solution.py:299
  1.8 0.3 collective-permute-start
  2.2 2.7 %collective-permute-done.refs_0_ = bf16[192,128]{1,0:T(8,128)(2,1)S(1)} collective-permute-done((bf16[192,128]{1,0:T(8,128)(2,1)S(1)}, bf16[192,128]{1,0:T(8,128)(2,1)S(1)}, u32[]{:S(2)}, u32[]{:S(2)}) %collective-permute-start) | collective-permute-done | bytes 49184 | tf_op jit(solution)/shard_map/ppermute | solution.py:309
  4.8 0.5 shard_map.65
  5.3 0.1 collective-permute-start.1
  5.4 1.3 %collective-permute-start.3 = (bf16[240,384]{1,0:T(8,128)(2,1)S(1)}, bf16[240,384]{1,0:T(8,128)(2,1)S(1)}, u32[]{:S(2)}, u32[]{:S(2)}) collective-permute-start(bf16[240,384]{1,0:T(8,128)(2,1)S(1)} %get-tuple-element.26), channel_id=1, source_target_pairs={{0,4},{4,8},{8,12},{12,0},{1,5},{5,9},{9,13},{13,1},{2,6},{6,10},{... | collective-permute-start | bytes 552968 | tf_op jit(solution)/shard_map/ppermute | solution.py:321
  6.7 1.1 %collective-permute-start.6 = (bf16[240,384]{1,0:T(8,128)(2,1)S(1)}, bf16[240,384]{1,0:T(8,128)(2,1)S(1)}, u32[]{:S(2)}, u32[]{:S(2)}) collective-permute-start(bf16[240,384]{1,0:T(8,128)(2,1)S(1)} %get-tuple-element.29), channel_id=1, source_target_pairs={{0,12},{4,0},{8,4},{12,8},{1,13},{5,1},{9,5},{13,9},{2,14},{6,2},{... | collective-permute-start | bytes 552968 | tf_op jit(solution)/shard_map/ppermute | solution.py:321
  7.9 2.4 %collective-permute-start.5 = (bf16[240,384]{1,0:T(8,128)(2,1)S(1)}, bf16[240,384]{1,0:T(8,128)(2,1)S(1)}, u32[]{:S(2)}, u32[]{:S(2)}) collective-permute-start(bf16[240,384]{1,0:T(8,128)(2,1)S(1)} %get-tuple-element.27.refs_0_), channel_id=1, source_target_pairs={{0,1},{1,0},{2,3},{3,2},{4,5},{5,4},{6,7},{7,6},{8,9},{9,8},{10,11... | collective-permute-start | bytes 552968 | tf_op jit(solution)/shard_map/ppermute | solution.py:279
  10.2 5.5 %collective-permute-done.1.refs_0_ = bf16[240,384]{1,0:T(8,128)(2,1)S(1)} collective-permute-done((bf16[240,384]{1,0:T(8,128)(2,1)S(1)}, bf16[240,384]{1,0:T(8,128)(2,1)S(1)}, u32[]{:S(2)}, u32[]{:S(2)}) %collective-permute-start.1) | collective-permute-done | bytes 184352 | tf_op jit(solution)/shard_map/ppermute | solution.py:321
  15.7 3.6 %collective-permute-start.2 = (bf16[240,384]{1,0:T(8,128)(2,1)S(1)}, bf16[240,384]{1,0:T(8,128)(2,1)S(1)}, u32[]{:S(2)}, u32[]{:S(2)}) collective-permute-start(bf16[240,384]{1,0:T(8,128)(2,1)S(1)} %collective-permute-done.1.refs_0_), channel_id=1, source_target_pairs={{0,1},{1,0},{2,3},{3,2},{4,5},{5,4},{6,7},{7,6},{8,9},{9,8},{10,11... | collective-permute-start | bytes 552968 | tf_op jit(solution)/shard_map/ppermute | solution.py:279
  19.3 5.1 %collective-permute-done.3.refs_0_ = bf16[240,384]{1,0:T(8,128)(2,1)S(1)} collective-permute-done((bf16[240,384]{1,0:T(8,128)(2,1)S(1)}, bf16[240,384]{1,0:T(8,128)(2,1)S(1)}, u32[]{:S(2)}, u32[]{:S(2)}) %collective-permute-start.3) | collective-permute-done | bytes 184352 | tf_op jit(solution)/shard_map/ppermute | solution.py:321
  24.4 0.8 %collective-permute-start.4 = (bf16[240,384]{1,0:T(8,128)(2,1)S(1)}, bf16[240,384]{1,0:T(8,128)(2,1)S(1)}, u32[]{:S(2)}, u32[]{:S(2)}) collective-permute-start(bf16[240,384]{1,0:T(8,128)(2,1)S(1)} %collective-permute-done.3.refs_0_), channel_id=1, source_target_pairs={{0,1},{1,0},{2,3},{3,2},{4,5},{5,4},{6,7},{7,6},{8,9},{9,8},{10,11... | collective-permute-start | bytes 552968 | tf_op jit(solution)/shard_map/ppermute | solution.py:279
  25.2 0.0 collective-permute-done.6.refs_0_
  25.2 0.0 collective-permute-start.7
  25.2 0.0 collective-permute-done.5.refs_1_
  25.2 3.2 %shard_map.66.refs_5_ = f32[4,224,192]{2,1,0:T(8,128)S(1)} custom-call(bf16[240,384]{1,0:T(8,128)(2,1)S(1)} %get-tuple-element.27.refs_0_, bf16[240,384]{1,0:T(8,128)(2,1)S(1)} %collective-permute-done.5.refs_1_, f32[384]{0:T(512)S(1)} %copy-done.3, bf16[27,192,384]{2,1,0:T(8,128)(2,1)S(1)} %bitcast.12, f32[1,192]{1,0:T(1,128)S(1)} %bitcast.18), custom_call_target="tpu_custom_call" | custom-call | flops 2378170368 | tf_op jit(solution)/shard_map/pallas_call | solution.py:398
  28.4 0.0 collective-permute-done.7.refs_1_
  28.5 3.3 %shard_map.68 = (bf16[1,224,384]{2,1,0:T(8,128)(2,1)S(1)}, f32[4,224,192]{2,1,0:T(8,128)S(1)}) custom-call(bf16[240,384]{1,0:T(8,128)(2,1)S(1)} %collective-permute-done.6.refs_0_, bf16[240,384]{1,0:T(8,128)(2,1)S(1)} %collective-permute-done.7.refs_1_, f32[384]{0:T(512)S(1)} %copy-done.3, bf16[27,192,384]{2,1,0:T(8,128)(2,1)S(1)} %bitcast.13, ...), custom_call_target="tpu_custom_call" | custom-call | flops 2378170368 | tf_op jit(solution)/shard_map/pallas_call | solution.py:398
  31.8 3.3 %shard_map.67 = (bf16[1,224,384]{2,1,0:T(8,128)(2,1)S(1)}, f32[4,224,192]{2,1,0:T(8,128)S(1)}) custom-call(bf16[240,384]{1,0:T(8,128)(2,1)S(1)} %collective-permute-done.3.refs_0_, bf16[240,384]{1,0:T(8,128)(2,1)S(1)} %collective-permute-done.4.refs_1_, f32[384]{0:T(512)S(1)} %copy-done.3, bf16[27,192,384]{2,1,0:T(8,128)(2,1)S(1)} %bitcast.14, ...), custom_call_target="tpu_custom_call" | custom-call | flops 2378170368 | tf_op jit(solution)/shard_map/pallas_call | solution.py:398
  35.1 0.0 collective-permute-done.2.refs_1_
  35.1 0.0 copy-start.1
  35.1 0.0 copy-start.5
  35.1 3.3 %shard_map.69.refs_0_ = bf16[2,224,384]{2,1,0:T(8,128)(2,1)S(1)} custom-call(bf16[240,384]{1,0:T(8,128)(2,1)S(1)} %collective-permute-done.1.refs_0_, bf16[240,384]{1,0:T(8,128)(2,1)S(1)} %collective-permute-done.2.refs_1_, f32[384]{0:T(512)S(1)} %copy-done.3, bf16[27,192,384]{2,1,0:T(8,128)(2,1)S(1)} %bitcast.15, f32[1,192]{1,0:T(1,128)S(1)} %bitcast.21, ...), custom_call_target="tpu_custom_call" | custom-call | flops 2378170368 | tf_op jit(solution)/shard_map/pallas_call | solution.py:398
  38.5 0.6 %collective-permute-start.8 = (bf16[2,224,384]{2,1,0:T(8,128)(2,1)S(1)}, bf16[2,224,384]{2,1,0:T(8,128)(2,1)S(1)}, u32[]{:S(2)}, u32[]{:S(2)}) collective-permute-start(bf16[2,224,384]{2,1,0:T(8,128)(2,1)S(1)} %shard_map.69.refs_0_), channel_id=1, source_target_pairs={{0,1},{1,0},{2,3},{3,2},{4,5},{5,4},{6,7},{7,6},{8,9},{9,8},{10,11... | collective-permute-start | bytes 1032200 | tf_op jit(solution)/shard_map/ppermute | solution.py:279
  39.0 0.1 collective-permute-start.10
  39.1 0.4 collective-permute-start.9
  39.6 0.9 %shard_map.70 = (bf16[2,3,256,768]{3,2,1,0:T(8,128)(2,1)S(1)}, f32[1,256]{1,0:T(1,128)S(1)}) custom-call(bf16[9,96,384]{2,1,0:T(8,128)(2,1)S(1)} %bitcast.16, f32[1,96]{1,0:T(1,128)S(1)} %bitcast.22), custom_call_target="tpu_custom_call" | custom-call | flops 1000000000 | tf_op jit(solution)/shard_map/pallas_call | solution.py:372
  40.4 0.1 collective-permute-done.10.refs_1_
  40.6 1.9 %shard_map.71.refs_4_ = bf16[8,5,48,192]{3,2,1,0:T(8,128)(2,1)} custom-call(bf16[1,224,384]{2,1,0:T(8,128)(2,1)S(1)} %get-tuple-element.34.refs_0_, bf16[1,224,384]{2,1,0:T(8,128)(2,1)S(1)} %collective-permute-done.10.refs_1_, bf16[2,3,256,768]{3,2,1,0:T(8,128)(2,1)S(1)} %get-tuple-element.31.refs_2_, f32[1,256]{1,0:T(1,128)S(1)} %get-tuple-element.32.refs_3_), custom_call_target="tpu_custom_call" | custom-call | flops 754974720 | tf_op jit(solution)/shard_map/pallas_call | solution.py:412
  42.4 1.9 %shard_map.72.refs_4_ = bf16[8,5,48,192]{3,2,1,0:T(8,128)(2,1)} custom-call(bf16[1,224,384]{2,1,0:T(8,128)(2,1)S(1)} %get-tuple-element.33.refs_0_, bf16[1,224,384]{2,1,0:T(8,128)(2,1)S(1)} %collective-permute-done.9.refs_1_, bf16[2,3,256,768]{3,2,1,0:T(8,128)(2,1)S(1)} %get-tuple-element.31.refs_2_, ...), custom_call_target="tpu_custom_call", output_to_operand_aliasing={{}: (4, {})} | custom-call | flops 754974720 | tf_op jit(solution)/shard_map/pallas_call | solution.py:412
  44.3 2.7 %shard_map.73 = bf16[8,5,48,192]{3,2,1,0:T(8,128)(2,1)} custom-call(bf16[2,224,384]{2,1,0:T(8,128)(2,1)S(1)} %shard_map.69.refs_0_, bf16[2,224,384]{2,1,0:T(8,128)(2,1)S(1)} %collective-permute-done.8.refs_1_, bf16[2,3,256,768]{3,2,1,0:T(8,128)(2,1)S(1)} %get-tuple-element.31.refs_2_, ...), custom_call_target="tpu_custom_call", output_to_operand_aliasing={{}: (4, {})} | custom-call | flops 1509949440 | tf_op jit(solution)/shard_map/pallas_call | solution.py:412
  (12 shorter events, 0.0 us)
Async XLA Ops:
  0.0 1.0 %copy-start.2 = (bf16[1,960,192]{1,2,0:T(8,128)(2,1)S(1)}, bf16[1,960,192]{1,2,0:T(8,128)(2,1)}, u32[]{:S(2)}) copy-start(bf16[1,960,192]{1,2,0:T(8,128)(2,1)} %param.6) | copy-start | bytes 1105924
  1.0 24.2 %copy-start = (bf16[3,3,3,384,192]{3,4,2,1,0:T(8,128)(2,1)S(1)}, bf16[3,3,3,384,192]{3,4,2,1,0:T(8,128)(2,1)}, u32[]{:S(2)}) copy-start(bf16[3,3,3,384,192]{3,4,2,1,0:T(8,128)(2,1)} %param.8) | copy-start | bytes 11943940
  1.0 24.2 %copy-start.3 = (f32[384]{0:T(512)S(1)}, f32[384]{0:T(512)}, u32[]{:S(2)}) copy-start(f32[384]{0:T(512)} %refs_2_.7) | copy-start | bytes 4612
  1.0 24.2 %copy-start.4 = (f32[192]{0:T(256)S(1)}, f32[192]{0:T(256)}, u32[]{:S(2)}) copy-start(f32[192]{0:T(256)} %param.9) | copy-start | bytes 2308
  1.8 3.0 %collective-permute-start = (bf16[192,128]{1,0:T(8,128)(2,1)S(1)}, bf16[192,128]{1,0:T(8,128)(2,1)S(1)}, u32[]{:S(2)}, u32[]{:S(2)}) collective-permute-start(bf16[192,128]{1,0:T(8,128)(2,1)S(1)} %get-tuple-element.20), channel_id=1, source_target_pairs={{0,2},{2,0},{1,3},{3,1},{4,6},{6,4},{5,7},{7,5},{8,10},{10,8},{9,1... | collective-permute-start | bytes 147464 | tf_op jit(solution)/shard_map/ppermute | solution.py:309
  5.3 10.4 %collective-permute-start.1 = (bf16[240,384]{1,0:T(8,128)(2,1)S(1)}, bf16[240,384]{1,0:T(8,128)(2,1)S(1)}, u32[]{:S(2)}, u32[]{:S(2)}) collective-permute-start(bf16[240,384]{1,0:T(8,128)(2,1)S(1)} %get-tuple-element.25), channel_id=1, source_target_pairs={{0,8},{4,12},{8,0},{12,4},{1,9},{5,13},{9,1},{13,5},{2,10},{6,14},... | collective-permute-start | bytes 552968 | tf_op jit(solution)/shard_map/ppermute | solution.py:321
  5.4 19.0 %collective-permute-start.3 = (bf16[240,384]{1,0:T(8,128)(2,1)S(1)}, bf16[240,384]{1,0:T(8,128)(2,1)S(1)}, u32[]{:S(2)}, u32[]{:S(2)}) collective-permute-start(bf16[240,384]{1,0:T(8,128)(2,1)S(1)} %get-tuple-element.26), channel_id=1, source_target_pairs={{0,4},{4,8},{8,12},{12,0},{1,5},{5,9},{9,13},{13,1},{2,6},{6,10},{... | collective-permute-start | bytes 552968 | tf_op jit(solution)/shard_map/ppermute | solution.py:321
  6.7 18.4 %collective-permute-start.6 = (bf16[240,384]{1,0:T(8,128)(2,1)S(1)}, bf16[240,384]{1,0:T(8,128)(2,1)S(1)}, u32[]{:S(2)}, u32[]{:S(2)}) collective-permute-start(bf16[240,384]{1,0:T(8,128)(2,1)S(1)} %get-tuple-element.29), channel_id=1, source_target_pairs={{0,12},{4,0},{8,4},{12,8},{1,13},{5,1},{9,5},{13,9},{2,14},{6,2},{... | collective-permute-start | bytes 552968 | tf_op jit(solution)/shard_map/ppermute | solution.py:321
  7.9 17.3 %collective-permute-start.5 = (bf16[240,384]{1,0:T(8,128)(2,1)S(1)}, bf16[240,384]{1,0:T(8,128)(2,1)S(1)}, u32[]{:S(2)}, u32[]{:S(2)}) collective-permute-start(bf16[240,384]{1,0:T(8,128)(2,1)S(1)} %get-tuple-element.27.refs_0_), channel_id=1, source_target_pairs={{0,1},{1,0},{2,3},{3,2},{4,5},{5,4},{6,7},{7,6},{8,9},{9,8},{10,11... | collective-permute-start | bytes 552968 | tf_op jit(solution)/shard_map/ppermute | solution.py:279
  15.7 19.4 %collective-permute-start.2 = (bf16[240,384]{1,0:T(8,128)(2,1)S(1)}, bf16[240,384]{1,0:T(8,128)(2,1)S(1)}, u32[]{:S(2)}, u32[]{:S(2)}) collective-permute-start(bf16[240,384]{1,0:T(8,128)(2,1)S(1)} %collective-permute-done.1.refs_0_), channel_id=1, source_target_pairs={{0,1},{1,0},{2,3},{3,2},{4,5},{5,4},{6,7},{7,6},{8,9},{9,8},{10,11... | collective-permute-start | bytes 552968 | tf_op jit(solution)/shard_map/ppermute | solution.py:279
  24.4 7.3 %collective-permute-start.4 = (bf16[240,384]{1,0:T(8,128)(2,1)S(1)}, bf16[240,384]{1,0:T(8,128)(2,1)S(1)}, u32[]{:S(2)}, u32[]{:S(2)}) collective-permute-start(bf16[240,384]{1,0:T(8,128)(2,1)S(1)} %collective-permute-done.3.refs_0_), channel_id=1, source_target_pairs={{0,1},{1,0},{2,3},{3,2},{4,5},{5,4},{6,7},{7,6},{8,9},{9,8},{10,11... | collective-permute-start | bytes 552968 | tf_op jit(solution)/shard_map/ppermute | solution.py:279
  25.2 3.3 %collective-permute-start.7 = (bf16[240,384]{1,0:T(8,128)(2,1)S(1)}, bf16[240,384]{1,0:T(8,128)(2,1)S(1)}, u32[]{:S(2)}, u32[]{:S(2)}) collective-permute-start(bf16[240,384]{1,0:T(8,128)(2,1)S(1)} %collective-permute-done.6.refs_0_), channel_id=1, source_target_pairs={{0,1},{1,0},{2,3},{3,2},{4,5},{5,4},{6,7},{7,6},{8,9},{9,8},{10,11... | collective-permute-start | bytes 552968 | tf_op jit(solution)/shard_map/ppermute | solution.py:279
  35.1 4.5 %copy-start.1 = (bf16[3,3,384,96]{2,3,1,0:T(8,128)(2,1)S(1)}, bf16[3,3,384,96]{2,3,1,0:T(8,128)(2,1)}, u32[]{:S(2)}) copy-start(bf16[3,3,384,96]{2,3,1,0:T(8,128)(2,1)} %param.10) | copy-start | bytes 1990660
  35.1 4.4 %copy-start.5 = (f32[96]{0:T(128)S(1)}, f32[96]{0:T(128)}, u32[]{:S(2)}) copy-start(f32[96]{0:T(128)} %param.11) | copy-start | bytes 1156
  38.5 5.8 %collective-permute-start.8 = (bf16[2,224,384]{2,1,0:T(8,128)(2,1)S(1)}, bf16[2,224,384]{2,1,0:T(8,128)(2,1)S(1)}, u32[]{:S(2)}, u32[]{:S(2)}) collective-permute-start(bf16[2,224,384]{2,1,0:T(8,128)(2,1)S(1)} %shard_map.69.refs_0_), channel_id=1, source_target_pairs={{0,1},{1,0},{2,3},{3,2},{4,5},{5,4},{6,7},{7,6},{8,9},{9,8},{10,11... | collective-permute-start | bytes 1032200 | tf_op jit(solution)/shard_map/ppermute | solution.py:279
  39.0 1.5 %collective-permute-start.10 = (bf16[1,224,384]{2,1,0:T(8,128)(2,1)S(1)}, bf16[1,224,384]{2,1,0:T(8,128)(2,1)S(1)}, u32[]{:S(2)}, u32[]{:S(2)}) collective-permute-start(bf16[1,224,384]{2,1,0:T(8,128)(2,1)S(1)} %get-tuple-element.34.refs_0_), channel_id=1, source_target_pairs={{0,1},{1,0},{2,3},{3,2},{4,5},{5,4},{6,7},{7,6},{8,9},{9,8},{10,11... | collective-permute-start | bytes 516104 | tf_op jit(solution)/shard_map/ppermute | solution.py:279
  39.1 3.3 %collective-permute-start.9 = (bf16[1,224,384]{2,1,0:T(8,128)(2,1)S(1)}, bf16[1,224,384]{2,1,0:T(8,128)(2,1)S(1)}, u32[]{:S(2)}, u32[]{:S(2)}) collective-permute-start(bf16[1,224,384]{2,1,0:T(8,128)(2,1)S(1)} %get-tuple-element.33.refs_0_), channel_id=1, source_target_pairs={{0,1},{1,0},{2,3},{3,2},{4,5},{5,4},{6,7},{7,6},{8,9},{9,8},{10,11... | collective-permute-start | bytes 516104 | tf_op jit(solution)/shard_map/ppermute | solution.py:279

commit v3 on v2

--- a/solution.py
+++ b/solution.py
@@ -11,7 +11,7 @@
 FRAMES = 8
 ROWS_DEV = 24
 PAIRS = FRAMES // 2
-ORDER = (0, 1, 3, 2)
+AHEAD = 2
 PITCH = 32
 HEAD = 8
 
@@ -61,61 +61,75 @@
     return jnp.where(lane == token, 1.0, 0.0).astype(bf16)
 
 
-def pack_kernel(count, cols, colors, x_ref, *outs):
-    seq, tile = lax.axis_index("seq"), lax.axis_index("tile")
-    width, span = cols + 4, count * cols
+def edge_kernel(span, colors, x_ref, *rest):
+    here_ref, outs = rest[0], rest[1:]
+    tile = lax.axis_index("tile")
     half = ROWS_DEV * span
     seg = round_up(2 * span, 64)
     chan = x_ref.shape[0]
-    rows = width * ROWS_DEV
+    here_ref[...] = x_ref[...]
     for color in range(colors):
         below = lax.rem(tile + color, 2) == 0
         parts = []
         for p in range(2):
-            last = x_ref[:, (p + 1) * half - 2 * span : (p + 1) * half]
-            first = x_ref[:, p * half : p * half + 2 * span]
+            last = here_ref[:, (p + 1) * half - 2 * span : (p + 1) * half]
+            first = here_ref[:, p * half : p * half + 2 * span]
             parts += [jnp.where(below, last, first), jnp.zeros((chan, seg - 2 * span), bf16)]
         outs[color][...] = jnp.concatenate(parts, axis=1)
+
+
+def pack_kernel(count, cols, x_ref, *outs):
+    seq = lax.axis_index("seq")
+    width, span = cols + 4, count * cols
+    half = ROWS_DEV * span
+    rows = width * ROWS_DEV
     for d in range(count):
-        pick = selection(rows, ROWS_DEV, width, cols, span, lax.rem(seq + d, count), half)
+        pick = selection(rows, ROWS_DEV, width, cols, span, jnp.bitwise_xor(seq, d), half)
         both = jnp.concatenate([dot_nt(pick, x_ref[:, p * half : (p + 1) * half]) for p in range(2)], axis=1)
-        outs[colors + d][0:rows, :] = both.astype(bf16)
+        outs[d][0:rows, :] = both.astype(bf16)
 
 
 def border_kernel(count, cols, colors, *refs):
+    late = [d for d in range(count) if d != AHEAD]
     edges = refs[:colors]
-    outs = refs[colors + count : colors + 2 * count]
-    held, sems = refs[colors + 2 * count :]
+    outs = refs[colors + len(late) : colors + 2 * len(late)]
+    ahead_ref, held, sems = refs[colors + 2 * len(late) :]
     seq = lax.axis_index("seq")
     width, span = cols + 4, count * cols
     rows = border_rows(width)
     seg = round_up(2 * span, 64)
-    picks = [selection(rows, 2, width, cols, span, lax.rem(seq + d, count), seg) for d in range(count)]
+    picks = [selection(rows, 2, width, cols, span, jnp.bitwise_xor(seq, d), seg) for d in range(count)]
     pick = jnp.concatenate(picks, axis=0)
     for color in range(colors):
         x = edges[color][...]
         both = jnp.concatenate([dot_nt(pick, x[:, p * seg : (p + 1) * seg]) for p in range(2)], axis=1)
         for d in range(count):
-            held[d, color * rows : (color + 1) * rows, :] = both[d * rows : (d + 1) * rows].astype(bf16)
+            piece = both[d * rows : (d + 1) * rows].astype(bf16)
+            if d == AHEAD:
+                ahead_ref[color * rows : (color + 1) * rows, :] = piece
+            else:
+                held[late.index(d), color * rows : (color + 1) * rows, :] = piece
     copies = []
-    for d in range(count):
-        to = outs[d].at[pl.ds(width * ROWS_DEV, colors * rows)]
-        copies.append(pltpu.make_async_copy(held.at[d], to, sems.at[d]))
+    for k in range(len(late)):
+        to = outs[k].at[pl.ds(width * ROWS_DEV, colors * rows)]
+        copies.append(pltpu.make_async_copy(held.at[k], to, sems.at[k]))
         copies[-1].start()
     for copy in copies:
         copy.wait()
 
 
 def conv_kernel(cfg, *refs):
-    width, kinds, ring, d, done = cfg
-    own_ref, other_ref, gain_ref, w_ref, bias_ref = refs[:5]
-    others = sorted({k for now, past in done for k in (now, past)} - {d})
-    parts = dict(zip(others, refs[5:]))
-    rest = refs[5 + len(others) :]
+    width, kinds, ring, d, pieces = cfg
+    gain_ref, w_ref, bias_ref = refs[:3]
+    mine_refs, their_refs = refs[3 : 3 + pieces], refs[3 + pieces : 3 + 2 * pieces]
+    refs = refs[3 + 2 * pieces :]
+    before = {1: 1, 3: 3}.get(d, 0)
+    parts = list(refs[:before])
+    rest = refs[before:]
     pad_ref, raw_ref, lhs_ref = rest[-3:]
-    mid_ref = rest[0] if done else None
-    part_ref = rest[1] if done else rest[0]
-    parts[d] = part_ref
+    mid_ref = rest[0] if d in (1, 3) else None
+    part_ref = rest[1] if d in (1, 3) else rest[0]
+    parts.append(part_ref)
     tile, chan_id, tiles = lax.axis_index("tile"), lax.axis_index("chan"), lax.axis_size("tile")
     seq, seqs = lax.axis_index("seq"), lax.axis_size("seq")
     chan = gain_ref.shape[0] // 2
@@ -132,15 +146,16 @@
             raw_ref[to, :] = raw[2 * w : 2 * w + 2]
 
     for p in range(2):
-        mine = own_ref[:, p * chan : (p + 1) * chan]
-        theirs = other_ref[:, p * chan : (p + 1) * chan]
+        lanes = slice(p * chan, (p + 1) * chan)
+        mine = jnp.concatenate([ref[:, lanes].astype(f32) for ref in mine_refs], axis=0)
+        theirs = jnp.concatenate([ref[:, lanes].astype(f32) for ref in their_refs], axis=0)
         low = jnp.where(chan_id == 0, mine, theirs)
         high = jnp.where(chan_id == 0, theirs, mine)
-        x = jnp.concatenate([low, high], axis=1).astype(f32)
+        x = jnp.concatenate([low, high], axis=1)
         scale = lax.rsqrt(jnp.mean(x * x, axis=-1, keepdims=True) + norm_eps)
         v = x * scale * gain
         act = v / (1.0 + jnp.exp(-v))
-        raw = mine.astype(f32)
+        raw = mine
         for w in range(width):
             to = slice(w * PITCH + HEAD, w * PITCH + HEAD + ROWS_DEV)
             pad_ref[to, :] = act[w * ROWS_DEV : (w + 1) * ROWS_DEV]
@@ -148,15 +163,15 @@
         tops, bottoms = [], []
         for k, kind in enumerate(kinds):
             at = main + k * border_rows(width)
-            pieces = raw[at : at + 2 * width], act[at : at + 2 * width]
+            cells = raw[at : at + 2 * width], act[at : at + 2 * width]
             if kind == "top":
-                tops.append(pieces)
+                tops.append(cells)
             elif kind == "bottom":
-                bottoms.append(pieces)
+                bottoms.append(cells)
             else:
                 below = lax.rem(tile + int(kind), 2) == 0
-                tops.append([jnp.where(below, 0.0, piece) for piece in pieces])
-                bottoms.append([jnp.where(below, piece, 0.0) for piece in pieces])
+                tops.append([jnp.where(below, 0.0, cell) for cell in cells])
+                bottoms.append([jnp.where(below, cell, 0.0) for cell in cells])
         for found, first in ((tops, HEAD - 2), (bottoms, HEAD + ROWS_DEV)):
             if found:
                 place(functools.reduce(jnp.add, [f[0] for f in found]), functools.reduce(jnp.add, [f[1] for f in found]), first)
@@ -182,17 +197,29 @@
             part_ref[2] += total[0]
             part_ref[3] = total[1]
 
-    if done:
+    if d in (1, 3):
         r = lax.broadcasted_iota(jnp.int32, (out_rows, 1), 0)
         h = jnp.bitwise_and(r, PITCH - 1) - 1
         good = (h >= jnp.where(tile == 0, 0, -1)) & (h < jnp.where(tile == tiles - 1, ROWS_DEV, ROWS_DEV + 1))
         good = good & (r >= jnp.where(seq == 0, PITCH, 0)) & (r < jnp.where(seq == seqs - 1, out_rows - PITCH, out_rows))
         base = seq if ring else 0
-        for k, (now, past) in enumerate(done):
-            first = lax.rem(base - now + PAIRS, PAIRS) == 0
+        odd = lax.rem(base, 2) == 1
+        high = base >= PAIRS // 2
+
+        def part(k, n):
+            pair = (parts[k - k % 2][n], parts[k - k % 2 + 1][n])
+            return jnp.where(odd, pair[1 - k % 2], pair[k % 2])
+
+        for k, pair in enumerate(((1,),) if d == 1 else ((0,), (2,), (3,))):
             mids = []
             for p in range(2):
-                value = parts[now][p] + jnp.where(first, 0.0, parts[past][2 + p]) + bias_ref[...]
+                value = part(pair[0], p) + bias_ref[...]
+                if pair[0] % 2:
+                    value = value + part(pair[0] - 1, 2 + p)
+                elif pair[0] == 0:
+                    value = value + jnp.where(high, part(3, 2 + p), 0.0)
+                else:
+                    value = value + jnp.where(high, 0.0, part(1, 2 + p))
                 mids.append(jnp.where(good, value, 0.0))
             mid_ref[k] = jnp.concatenate(mids, axis=1).astype(bf16)
 
@@ -224,11 +251,24 @@
 
 
 def up_kernel(cfg, *refs):
-    mid_w, ring, shifts = cfg
+    mid_w, ring, final = cfg
     own_ref, other_ref, w_ref, bias_ref = refs[:4]
-    out_ref, lhs_ref, rows_ref, held_ref, sems = refs[-5:]
+    if final:
+        first_ref, out_ref, lhs_ref, rows_ref, held_ref, sems = refs[4:]
+    else:
+        held_ref, lhs_ref, rows_ref = refs[4:]
     chan_id = lax.axis_index("chan")
-    base = lax.axis_index("seq") if ring else 0
+    copies = []
+
+    def write(source, pair, sem):
+        base = lax.axis_index("seq") if ring else 0
+        half = jnp.where(base >= PAIRS // 2, PAIRS // 2, 0)
+        frame = 2 * (half + pair if pair < 2 else PAIRS // 2 - half + pair - 2)
+        copies.append(pltpu.make_async_copy(source, out_ref.at[pl.ds(frame, 2)], sem))
+        copies[-1].start()
+
+    if final:
+        write(first_ref, 1, sems.at[0])
     chan = own_ref.shape[2] // 2
     cols = mid_w - 2
     keep = (mid_w - 1) * PITCH + ROWS_DEV
@@ -262,15 +302,13 @@
                     piece = total[f, w * PITCH : w * PITCH + ROWS_DEV, k * 128 : (k + 1) * 128]
                     rows_ref[k, f * cols + w, pl.ds(i, ROWS_DEV, stride=2), :] = piece
     bias = bias_ref[:, : held_ref.shape[3]]
-    copies = []
     for k in range(count):
         for f in (2 * k, 2 * k + 1):
             for w in range(cols):
                 row = jnp.concatenate([rows_ref[c, f * cols + w] for c in range(lanes // 128)], axis=1)
                 held_ref[f, w] = (row[:, : held_ref.shape[3]] + bias).astype(bf16)
-        frame = 2 * lax.rem(base - shifts[k] + PAIRS, PAIRS)
-        copies.append(pltpu.make_async_copy(held_ref.at[pl.ds(2 * k, 2)], out_ref.at[pl.ds(frame, 2)], sems.at[k]))
-        copies[-1].start()
+        if final:
+            write(held_ref.at[pl.ds(2 * k, 2)], (0, 2, 3)[k], sems.at[1 + k])
     for copy in copies:
         copy.wait()
 
@@ -286,7 +324,7 @@
     return out
 
 
-def arrive_by_ring(latents, cols):
+def arrive_by_trade(latents, cols):
     seqs, tiles = lax.axis_size("seq"), lax.axis_size("tile")
     colors = min(2, tiles - 1)
     width, span = cols + 4, cols * seqs
@@ -296,29 +334,31 @@
     rows = width * ROWS_DEV + colors * border
     edge = jax.ShapeDtypeStruct((chan, 2 * round_up(2 * span, 64)), bf16)
     block = jax.ShapeDtypeStruct((rows, 2 * chan), bf16)
-    packed = call(
-        functools.partial(pack_kernel, seqs, cols, colors),
-        [edge] * colors + [block] * seqs,
-        [VM],
-        [VM] * (colors + seqs),
-        [],
-        12,
-        flops=2 * 10**9,
+    whole = jax.ShapeDtypeStruct(x.shape, bf16)
+    bare = jax.ShapeDtypeStruct((width * ROWS_DEV, 2 * chan), bf16)
+    outs = [bare if d == AHEAD else block for d in range(seqs)]
+    late = [d for d in range(seqs) if d != AHEAD]
+    here, *edges = call(
+        functools.partial(edge_kernel, span, colors), [whole] + [edge] * colors, [VM], [VM] * (1 + colors), [], 4
     )(x)
-    edges, windows = packed[:colors], packed[colors:]
+    windows = call(functools.partial(pack_kernel, seqs, cols), outs, [VM], [VM] * seqs, [], 12, flops=2 * 10**9)(here)
     edges = [lax.ppermute(e, "tile", tile_pairs(color, tiles)) for color, e in enumerate(edges)]
-    windows = call(
+    *done, borders = call(
         functools.partial(border_kernel, seqs, cols, colors),
-        [block] * seqs,
-        [VM] * colors + [ANY] * seqs,
-        [ANY] * seqs,
-        [pltpu.VMEM((seqs, colors * border, 2 * chan), bf16), pltpu.SemaphoreType.DMA((seqs,))],
+        [block] * len(late) + [jax.ShapeDtypeStruct((colors * border, 2 * chan), bf16)],
+        [VM] * colors + [ANY] * len(late),
+        [ANY] * len(late) + [VM],
+        [pltpu.VMEM((len(late), colors * border, 2 * chan), bf16), pltpu.SemaphoreType.DMA((len(late),))],
         4,
-        aliases={colors + d: d for d in range(seqs)},
-    )(*edges, *windows)
-    blocks = [windows[0]]
+        aliases={colors + k: k for k in range(len(late))},
+    )(*edges, *[windows[d] for d in late])
+
+    def trade(x, d):
+        return lax.ppermute(x, "seq", [(i, i ^ d) for i in range(seqs)])
+
+    blocks = [(done[0],)]
     for d in range(1, seqs):
-        blocks.append(lax.ppermute(windows[d], "seq", [(i, (i + d) % seqs) for i in range(seqs)]))
+        blocks.append((trade(windows[d], d), trade(borders, d)) if d == AHEAD else (trade(done[late.index(d)], d),))
     return blocks, [str(c) for c in range(colors)]
 
 
@@ -352,10 +392,9 @@
     spare = ((0, border_rows(width) - 2 * width), (0, 0))
     blocks = []
     for d in range(PAIRS):
-        k = -d % PAIRS
-        pieces = [paired[k, :, 2:-2].reshape(-1, 2 * chan)]
-        pieces += [jnp.pad(b.reshape(-1, 2 * chan), spare) for b in (paired[k, :, :2], paired[k, :, -2:])]
-        blocks.append(jnp.concatenate(pieces, axis=0))
+        pieces = [paired[d, :, 2:-2].reshape(-1, 2 * chan)]
+        pieces += [jnp.pad(b.reshape(-1, 2 * chan), spare) for b in (paired[d, :, :2], paired[d, :, -2:])]
+        blocks.append((jnp.concatenate(pieces, axis=0),))
     return blocks, ["top", "bottom"]
 
 
@@ -365,7 +404,7 @@
     width, mid_w = cols + 4, cols + 2
     out_rows = mid_w * PITCH
     ring = 2 * lax.axis_size("seq") == FRAMES
-    blocks, kinds = arrive_by_ring(latents, cols) if ring else arrive_by_all_to_all(latents, cols)
+    blocks, kinds = arrive_by_trade(latents, cols) if ring else arrive_by_all_to_all(latents, cols)
 
     up_lanes = round_up(2 * out_chan, 128)
     taps = upsample_weight.transpose(0, 1, 3, 2).reshape(9, out_chan, 2 * chan)
@@ -388,52 +427,46 @@
         pltpu.VMEM((2, width * PITCH, 6 * chan), bf16),
     ]
 
-    def conv(d, parts=None, done=()):
-        keep = d != ORDER[-1]
-        others = sorted({k for pair in done for k in pair} - {d})
-        before = [parts[k] for k in others]
-        outs = [jax.ShapeDtypeStruct((len(done), out_rows, 2 * chan), bf16)] if done else []
-        outs += [part] if keep else []
-        other = swap_chan(blocks[d])
+    def conv(d, *before):
+        outs = [jax.ShapeDtypeStruct((d, out_rows, 2 * chan), bf16)] if d in (1, 3) else []
+        outs += [part] if d < 3 else []
+        others = [swap_chan(block) for block in blocks[d]]
         return call(
-            functools.partial(conv_kernel, (width, kinds, ring, d, done)),
+            functools.partial(conv_kernel, (width, kinds, ring, d, len(others))),
             outs,
-            [VM] * (5 + len(before)),
+            [VM] * (3 + 2 * len(others) + len(before)),
             [VM] * len(outs),
-            ([] if keep else [pltpu.VMEM((4, out_rows, chan), f32)]) + work,
+            ([] if d < 3 else [pltpu.VMEM((4, out_rows, chan), f32)]) + work,
             14,
             flops=2 * 2 * out_rows * 27 * 2 * chan * 256,
-        )(blocks[d], other, gain, weights, bias, *before)
-
-    def upsample(mids, shifts, out=None):
-        held = () if out is None else (out,)
-        count = len(shifts)
+        )(gain, weights, bias, *blocks[d], *others, *before)
+
+    def upsample(mids, *early):
+        count, final = mids.shape[0], len(early)
+        held = (2 * count, cols, 2 * ROWS_DEV, 2 * out_chan)
+        scratch = [
+            pltpu.VMEM((2 * count, out_rows, 6 * chan), bf16),
+            pltpu.VMEM((up_lanes // 128, 2 * count * cols, 2 * ROWS_DEV, 128), f32),
+        ]
+        if final:
+            scratch += [pltpu.VMEM(held, bf16), pltpu.SemaphoreType.DMA((1 + count,))]
         other = swap_chan(mids)
         return call(
-            functools.partial(up_kernel, (mid_w, ring, shifts)),
-            jax.ShapeDtypeStruct((FRAMES, cols, 2 * ROWS_DEV, 2 * out_chan), bf16),
-            [VM] * 4 + [ANY] * len(held),
-            ANY,
-            [
-                pltpu.VMEM((2 * count, out_rows, 6 * chan), bf16),
-                pltpu.VMEM((up_lanes // 128, 2 * count * cols, 2 * ROWS_DEV, 128), f32),
-                pltpu.VMEM((2 * count, cols, 2 * ROWS_DEV, 2 * out_chan), bf16),
-                pltpu.SemaphoreType.DMA((count,)),
-            ],
+            functools.partial(up_kernel, (mid_w, ring, final)),
+            jax.ShapeDtypeStruct((FRAMES, *held[1:]) if final else held, bf16),
+            [VM] * (4 + final),
+            ANY if final else VM,
+            scratch,
             14,
             flops=2 * 2 * 2 * count * cols * PITCH * 12 * chan * 256,
-            aliases={4: 0} if held else None,
-        )(mids, other, up_weights, up_bias, *held)
-
-    parts = {}
-    (parts[0],) = conv(0)
-    mid0, parts[1] = conv(1, parts, ((0, 1),))
-    mid3, parts[3] = conv(3, parts, ((3, 0),))
-    decoded = upsample(mid0, (0,))
-    decoded = upsample(mid3, (3,), decoded)
-    (late,) = conv(2, parts, ((1, 2), (2, 3)))
-    decoded = upsample(late, (1, 2), decoded)
-    return decoded.transpose(0, 2, 1, 3)
+        )(mids, other, up_weights, up_bias, *early)
+
+    (part0,) = conv(0)
+    early, part1 = conv(1, part0)
+    first = upsample(early)
+    (part2,) = conv(2)
+    (late,) = conv(3, part0, part1, part2)
+    return upsample(late, first).transpose(0, 2, 1, 3)
 
 
 def solution(mesh):

time: 47.2 us -> 47.3 us (level)
  the two profiles are of different devices: /device:TPU:23 before, /device:TPU:0 now
where the time goes in v3:
time: 47.3 us; the launch traced here: 47.1 us
  Pallas kernels  20.6 us (44%)
  waiting for transfers between devices  13.6 us (29%)
  starting transfers between devices  11.8 us (25%)
  local copies, waits for them, and re-layouts  1.02 us (2%)
    pallas_call x4, Pallas kernels, conv(): call(functools.partial(conv_kernel, (width, kinds, ring, d, len(others)))...  13.4 us
    ppermute x4, waiting for transfers between devices, trade(): return lax.ppermute(x, 'seq', [(i, i ^ d) for i in range(seqs)])  11.6 us
    ppermute x4, starting transfers between devices, trade(): return lax.ppermute(x, 'seq', [(i, i ^ d) for i in range(seqs)])  7.12 us
    pallas_call x2, Pallas kernels, upsample(): call(functools.partial(up_kernel, (mid_w, ring, final)), jax.ShapeDtypeSt...  4.91 us
    ppermute x1, starting transfers between devices, arrive_by_trade(): lax.ppermute(e, 'tile', tile_pairs(color, tiles))  3.03 us
    ppermute x7, starting transfers between devices, swap_chan(): return lax.ppermute(x, 'chan', [(0, 1), (1, 0)])  1.6 us
    ppermute x1, waiting for transfers between devices, arrive_by_trade(): lax.ppermute(e, 'tile', tile_pairs(color, tiles))  1.26 us
    unnamed x12, local copies, waits for them, and re-layouts  1.02 us
  transfers between devices with their start and end apart: 12, of which 3 were waited for; matrix products, arithmetic and copies ran while one was open for 0% of the time, Pallas kernels for 27%

profile of v3, /device:TPU:0, one launch (start us, length us, event | category | flops | bytes accessed | tf_op | source)
XLA Modules:
  0.0 47.1 jit_solution(2178809120837801232)
XLA Ops:
  0.0 1.0 %copy-done = bf16[1,960,192]{1,2,0:T(8,128)(2,1)S(1)} copy-done((bf16[1,960,192]{1,2,0:T(8,128)(2,1)S(1)}, bf16[1,960,192]{1,2,0:T(8,128)(2,1)}, u32[]{:S(2)}) %copy-start) | copy-done | bytes 368664
  1.0 0.2 shard_map.64
  1.2 3.0 %collective-permute-start = (bf16[192,128]{1,0:T(8,128)(2,1)S(1)}, bf16[192,128]{1,0:T(8,128)(2,1)S(1)}, u32[]{:S(2)}, u32[]{:S(2)}) collective-permute-start(bf16[192,128]{1,0:T(8,128)(2,1)S(1)} %get-tuple-element.19), channel_id=1, source_target_pairs={{0,2},{2,0},{1,3},{3,1},{4,6},{6,4},{5,7},{7,5},{8,10},{10,8},{9,1... | collective-permute-start | bytes 147464 | tf_op jit(solution)/shard_map/ppermute | solution.py:345
  4.2 0.8 %shard_map.65 = (bf16[240,384]{1,0:T(8,128)(2,1)S(1)}, bf16[240,384]{1,0:T(8,128)(2,1)S(1)}, bf16[216,384]{1,0:T(8,128)(2,1)S(1)}, bf16[240,384]{1,0:T(8,128)(2,1)S(1)}) custom-call(bf16[192,960]{1,0:T(8,128)(2,1)S(1)} %get-tuple-element.20.x_ref), custom_call_target="tpu_custom_call" | custom-call | flops 2000000000 | tf_op jit(solution)/shard_map/pallas_call | solution.py:344
  5.1 1.3 %collective-permute-done.refs_0_ = bf16[192,128]{1,0:T(8,128)(2,1)S(1)} collective-permute-done((bf16[192,128]{1,0:T(8,128)(2,1)S(1)}, bf16[192,128]{1,0:T(8,128)(2,1)S(1)}, u32[]{:S(2)}, u32[]{:S(2)}) %collective-permute-start) | collective-permute-done | bytes 49184 | tf_op jit(solution)/shard_map/ppermute | solution.py:345
  6.3 0.4 shard_map.66
  6.7 4.2 %collective-permute-start.1 = (bf16[240,384]{1,0:T(8,128)(2,1)S(1)}, bf16[240,384]{1,0:T(8,128)(2,1)S(1)}, u32[]{:S(2)}, u32[]{:S(2)}) collective-permute-start(bf16[240,384]{1,0:T(8,128)(2,1)S(1)} %get-tuple-element.24), channel_id=1, source_target_pairs={{0,12},{4,8},{8,4},{12,0},{1,13},{5,9},{9,5},{13,1},{2,14},{6,10},... | collective-permute-start | bytes 552968 | tf_op jit(solution)/shard_map/ppermute | solution.py:357
  10.9 0.0 collective-permute-start.4
  10.9 0.6 %collective-permute-start.6 = (bf16[216,384]{1,0:T(8,128)(2,1)S(1)}, bf16[216,384]{1,0:T(8,128)(2,1)S(1)}, u32[]{:S(2)}, u32[]{:S(2)}) collective-permute-start(bf16[216,384]{1,0:T(8,128)(2,1)S(1)} %get-tuple-element.28), channel_id=1, source_target_pairs={{0,8},{4,12},{8,0},{12,4},{1,9},{5,13},{9,1},{13,5},{2,10},{6,14},... | collective-permute-start | bytes 497672 | tf_op jit(solution)/shard_map/ppermute | solution.py:357
  11.6 2.3 %collective-permute-start.7 = (bf16[24,384]{1,0:T(8,128)(2,1)S(1)}, bf16[24,384]{1,0:T(8,128)(2,1)S(1)}, u32[]{:S(2)}, u32[]{:S(2)}) collective-permute-start(bf16[24,384]{1,0:T(8,128)(2,1)S(1)} %get-tuple-element.29), channel_id=1, source_target_pairs={{0,8},{4,12},{8,0},{12,4},{1,9},{5,13},{9,1},{13,5},{2,10},{6,14},... | collective-permute-start | bytes 55304 | tf_op jit(solution)/shard_map/ppermute | solution.py:357
  13.9 11.6 %collective-permute-done.7.refs_4_ = bf16[24,384]{1,0:T(8,128)(2,1)S(1)} collective-permute-done((bf16[24,384]{1,0:T(8,128)(2,1)S(1)}, bf16[24,384]{1,0:T(8,128)(2,1)S(1)}, u32[]{:S(2)}, u32[]{:S(2)}) %collective-permute-start.7) | collective-permute-done | bytes 18464 | tf_op jit(solution)/shard_map/ppermute | solution.py:357
  25.4 0.0 collective-permute-start.9
  25.4 0.0 collective-permute-done.6.refs_3_
  25.4 0.5 %collective-permute-start.8 = (bf16[216,384]{1,0:T(8,128)(2,1)S(1)}, bf16[216,384]{1,0:T(8,128)(2,1)S(1)}, u32[]{:S(2)}, u32[]{:S(2)}) collective-permute-start(bf16[216,384]{1,0:T(8,128)(2,1)S(1)} %collective-permute-done.6.refs_3_), channel_id=1, source_target_pairs={{0,1},{1,0},{2,3},{3,2},{4,5},{5,4},{6,7},{7,6},{8,9},{9,8},{10,11... | collective-permute-start | bytes 497672 | tf_op jit(solution)/shard_map/ppermute | solution.py:317
  25.9 0.0 collective-permute-done.1.refs_3_
  25.9 0.1 collective-permute-start.2
  26.0 0.0 collective-permute-done.4.refs_3_
  26.0 0.4 collective-permute-start.5
  26.5 0.0 collective-permute-done.3.refs_4_
  26.5 3.2 %shard_map.67.refs_5_ = f32[4,224,192]{2,1,0:T(8,128)S(1)} custom-call(f32[384]{0:T(512)S(1)} %copy-done.3, bf16[27,192,384]{2,1,0:T(8,128)(2,1)S(1)} %bitcast.13, f32[1,192]{1,0:T(1,128)S(1)} %bitcast.18, bf16[240,384]{1,0:T(8,128)(2,1)S(1)} %get-tuple-element.25.refs_3_, bf16[240,384]{1,0:T(8,128)(2,1)S(1)} %collective-permute-done.3.refs_4_), custom_call_target="tpu_custom_call" | custom-call | flops 2378170368 | tf_op jit(solution)/shard_map/pallas_call | solution.py:434
  29.7 0.0 collective-permute-done.9.refs_6_
  29.8 3.2 %shard_map.69.refs_7_ = f32[4,224,192]{2,1,0:T(8,128)S(1)} custom-call(f32[384]{0:T(512)S(1)} %copy-done.3, bf16[27,192,384]{2,1,0:T(8,128)(2,1)S(1)} %bitcast.14, f32[1,192]{1,0:T(1,128)S(1)} %bitcast.19, bf16[216,384]{1,0:T(8,128)(2,1)S(1)} %collective-permute-done.6.refs_3_, bf16[24,384]{1,0:T(8,128)(2,1)S(1)} %collective-permute-done.7.refs_4_, ...), custom_call_target="tpu_custom_call" | custom-call | flops 2378170368 | tf_op jit(solution)/shard_map/pallas_call | solution.py:434
  33.0 3.4 %shard_map.68 = (bf16[1,224,384]{2,1,0:T(8,128)(2,1)S(1)}, f32[4,224,192]{2,1,0:T(8,128)S(1)}) custom-call(f32[384]{0:T(512)S(1)} %copy-done.3, bf16[27,192,384]{2,1,0:T(8,128)(2,1)S(1)} %bitcast.15, f32[1,192]{1,0:T(1,128)S(1)} %bitcast.20, bf16[240,384]{1,0:T(8,128)(2,1)S(1)} %collective-permute-done.4.refs_3_, ...), custom_call_target="tpu_custom_call" | custom-call | flops 2378170368 | tf_op jit(solution)/shard_map/pallas_call | solution.py:434
  36.4 0.0 copy-start.2
  36.4 0.0 copy-start.5
  36.4 3.5 %shard_map.70.refs_0_ = bf16[3,224,384]{2,1,0:T(8,128)(2,1)S(1)} custom-call(f32[384]{0:T(512)S(1)} %copy-done.3, bf16[27,192,384]{2,1,0:T(8,128)(2,1)S(1)} %bitcast.16, f32[1,192]{1,0:T(1,128)S(1)} %bitcast.21, bf16[240,384]{1,0:T(8,128)(2,1)S(1)} %collective-permute-done.1.refs_3_, bf16[240,384]{1,0:T(8,128)(2,1)S(1)} %collective-permute-done.2.refs_4_, ...), custom_call_target="tpu_custom_call" | custom-call | flops 2378170368 | tf_op jit(solution)/shard_map/pallas_call | solution.py:434
  40.0 0.1 collective-permute-start.10
  40.1 0.4 collective-permute-start.11
  40.6 0.9 %shard_map.71 = (bf16[2,3,256,768]{3,2,1,0:T(8,128)(2,1)S(1)}, f32[1,256]{1,0:T(1,128)S(1)}) custom-call(bf16[9,96,384]{2,1,0:T(8,128)(2,1)S(1)} %bitcast.17, f32[1,96]{1,0:T(1,128)S(1)} %bitcast.22), custom_call_target="tpu_custom_call" | custom-call | flops 1000000000 | tf_op jit(solution)/shard_map/pallas_call | solution.py:411
  41.5 0.7 %collective-permute-done.11.refs_1_ = bf16[1,224,384]{2,1,0:T(8,128)(2,1)S(1)} collective-permute-done((bf16[1,224,384]{2,1,0:T(8,128)(2,1)S(1)}, bf16[1,224,384]{2,1,0:T(8,128)(2,1)S(1)}, u32[]{:S(2)}, u32[]{:S(2)}) %collective-permute-start.11) | collective-permute-done | bytes 172064 | tf_op jit(solution)/shard_map/ppermute | solution.py:317
  42.2 1.2 %shard_map.72.refs_4_ = bf16[2,5,48,192]{3,2,1,0:T(8,128)(2,1)S(1)} custom-call(bf16[1,224,384]{2,1,0:T(8,128)(2,1)S(1)} %get-tuple-element.32.refs_0_, bf16[1,224,384]{2,1,0:T(8,128)(2,1)S(1)} %collective-permute-done.11.refs_1_, bf16[2,3,256,768]{3,2,1,0:T(8,128)(2,1)S(1)} %get-tuple-element.30.refs_2_, f32[1,256]{1,0:T(1,128)S(1)} %get-tuple-element.31.refs_3_), custom_call_target="tpu_custom_call" | custom-call | flops 754974720 | tf_op jit(solution)/shard_map/pallas_call | solution.py:454
  43.4 3.8 %shard_map.73 = bf16[8,5,48,192]{3,2,1,0:T(8,128)(2,1)} custom-call(bf16[3,224,384]{2,1,0:T(8,128)(2,1)S(1)} %shard_map.70.refs_0_, bf16[3,224,384]{2,1,0:T(8,128)(2,1)S(1)} %collective-permute-done.10.refs_1_, bf16[2,3,256,768]{3,2,1,0:T(8,128)(2,1)S(1)} %get-tuple-element.30.refs_2_, f32[1,256]{1,0:T(1,128)S(1)} %get-tuple-element.31.refs_3_, ...), custom_call_target="tpu_custom_call" | custom-call | flops 2264924160 | tf_op jit(solution)/shard_map/pallas_call | solution.py:454
  (14 shorter events, 0.0 us)
Async XLA Ops:
  0.0 1.0 %copy-start = (bf16[1,960,192]{1,2,0:T(8,128)(2,1)S(1)}, bf16[1,960,192]{1,2,0:T(8,128)(2,1)}, u32[]{:S(2)}) copy-start(bf16[1,960,192]{1,2,0:T(8,128)(2,1)} %param.6) | copy-start | bytes 1105924
  1.2 5.1 %collective-permute-start = (bf16[192,128]{1,0:T(8,128)(2,1)S(1)}, bf16[192,128]{1,0:T(8,128)(2,1)S(1)}, u32[]{:S(2)}, u32[]{:S(2)}) collective-permute-start(bf16[192,128]{1,0:T(8,128)(2,1)S(1)} %get-tuple-element.19), channel_id=1, source_target_pairs={{0,2},{2,0},{1,3},{3,1},{4,6},{6,4},{5,7},{7,5},{8,10},{10,8},{9,1... | collective-permute-start | bytes 147464 | tf_op jit(solution)/shard_map/ppermute | solution.py:345
  4.2 22.2 %copy-start.1 = (bf16[3,3,3,384,192]{3,4,2,1,0:T(8,128)(2,1)S(1)}, bf16[3,3,3,384,192]{3,4,2,1,0:T(8,128)(2,1)}, u32[]{:S(2)}) copy-start(bf16[3,3,3,384,192]{3,4,2,1,0:T(8,128)(2,1)} %param.8) | copy-start | bytes 11943940
  4.2 22.2 %copy-start.3 = (f32[384]{0:T(512)S(1)}, f32[384]{0:T(512)}, u32[]{:S(2)}) copy-start(f32[384]{0:T(512)} %refs_0_.7) | copy-start | bytes 4612
  4.2 22.2 %copy-start.4 = (f32[192]{0:T(256)S(1)}, f32[192]{0:T(256)}, u32[]{:S(2)}) copy-start(f32[192]{0:T(256)} %param.9) | copy-start | bytes 2308
  6.7 19.2 %collective-permute-start.1 = (bf16[240,384]{1,0:T(8,128)(2,1)S(1)}, bf16[240,384]{1,0:T(8,128)(2,1)S(1)}, u32[]{:S(2)}, u32[]{:S(2)}) collective-permute-start(bf16[240,384]{1,0:T(8,128)(2,1)S(1)} %get-tuple-element.24), channel_id=1, source_target_pairs={{0,12},{4,8},{8,4},{12,0},{1,13},{5,9},{9,5},{13,1},{2,14},{6,10},... | collective-permute-start | bytes 552968 | tf_op jit(solution)/shard_map/ppermute | solution.py:357
  10.9 15.1 %collective-permute-start.4 = (bf16[240,384]{1,0:T(8,128)(2,1)S(1)}, bf16[240,384]{1,0:T(8,128)(2,1)S(1)}, u32[]{:S(2)}, u32[]{:S(2)}) collective-permute-start(bf16[240,384]{1,0:T(8,128)(2,1)S(1)} %get-tuple-element.26), channel_id=1, source_target_pairs={{0,4},{4,0},{8,12},{12,8},{1,5},{5,1},{9,13},{13,9},{2,6},{6,2},{1... | collective-permute-start | bytes 552968 | tf_op jit(solution)/shard_map/ppermute | solution.py:357
  10.9 15.5 %collective-permute-start.3 = (bf16[240,384]{1,0:T(8,128)(2,1)S(1)}, bf16[240,384]{1,0:T(8,128)(2,1)S(1)}, u32[]{:S(2)}, u32[]{:S(2)}) collective-permute-start(bf16[240,384]{1,0:T(8,128)(2,1)S(1)} %get-tuple-element.25.refs_3_), channel_id=1, source_target_pairs={{0,1},{1,0},{2,3},{3,2},{4,5},{5,4},{6,7},{7,6},{8,9},{9,8},{10,11... | collective-permute-start | bytes 552968 | tf_op jit(solution)/shard_map/ppermute | solution.py:317
  10.9 14.5 %collective-permute-start.6 = (bf16[216,384]{1,0:T(8,128)(2,1)S(1)}, bf16[216,384]{1,0:T(8,128)(2,1)S(1)}, u32[]{:S(2)}, u32[]{:S(2)}) collective-permute-start(bf16[216,384]{1,0:T(8,128)(2,1)S(1)} %get-tuple-element.28), channel_id=1, source_target_pairs={{0,8},{4,12},{8,0},{12,4},{1,9},{5,13},{9,1},{13,5},{2,10},{6,14},... | collective-permute-start | bytes 497672 | tf_op jit(solution)/shard_map/ppermute | solution.py:357
  11.6 13.8 %collective-permute-start.7 = (bf16[24,384]{1,0:T(8,128)(2,1)S(1)}, bf16[24,384]{1,0:T(8,128)(2,1)S(1)}, u32[]{:S(2)}, u32[]{:S(2)}) collective-permute-start(bf16[24,384]{1,0:T(8,128)(2,1)S(1)} %get-tuple-element.29), channel_id=1, source_target_pairs={{0,8},{4,12},{8,0},{12,4},{1,9},{5,13},{9,1},{13,5},{2,10},{6,14},... | collective-permute-start | bytes 55304 | tf_op jit(solution)/shard_map/ppermute | solution.py:357
  25.4 4.3 %collective-permute-start.9 = (bf16[24,384]{1,0:T(8,128)(2,1)S(1)}, bf16[24,384]{1,0:T(8,128)(2,1)S(1)}, u32[]{:S(2)}, u32[]{:S(2)}) collective-permute-start(bf16[24,384]{1,0:T(8,128)(2,1)S(1)} %collective-permute-done.7.refs_4_), channel_id=1, source_target_pairs={{0,1},{1,0},{2,3},{3,2},{4,5},{5,4},{6,7},{7,6},{8,9},{9,8},{10,11... | collective-permute-start | bytes 55304 | tf_op jit(solution)/shard_map/ppermute | solution.py:317
  25.4 4.3 %collective-permute-start.8 = (bf16[216,384]{1,0:T(8,128)(2,1)S(1)}, bf16[216,384]{1,0:T(8,128)(2,1)S(1)}, u32[]{:S(2)}, u32[]{:S(2)}) collective-permute-start(bf16[216,384]{1,0:T(8,128)(2,1)S(1)} %collective-permute-done.6.refs_3_), channel_id=1, source_target_pairs={{0,1},{1,0},{2,3},{3,2},{4,5},{5,4},{6,7},{7,6},{8,9},{9,8},{10,11... | collective-permute-start | bytes 497672 | tf_op jit(solution)/shard_map/ppermute | solution.py:317
  25.9 10.5 %collective-permute-start.2 = (bf16[240,384]{1,0:T(8,128)(2,1)S(1)}, bf16[240,384]{1,0:T(8,128)(2,1)S(1)}, u32[]{:S(2)}, u32[]{:S(2)}) collective-permute-start(bf16[240,384]{1,0:T(8,128)(2,1)S(1)} %collective-permute-done.1.refs_3_), channel_id=1, source_target_pairs={{0,1},{1,0},{2,3},{3,2},{4,5},{5,4},{6,7},{7,6},{8,9},{9,8},{10,11... | collective-permute-start | bytes 552968 | tf_op jit(solution)/shard_map/ppermute | solution.py:317
  26.0 7.0 %collective-permute-start.5 = (bf16[240,384]{1,0:T(8,128)(2,1)S(1)}, bf16[240,384]{1,0:T(8,128)(2,1)S(1)}, u32[]{:S(2)}, u32[]{:S(2)}) collective-permute-start(bf16[240,384]{1,0:T(8,128)(2,1)S(1)} %collective-permute-done.4.refs_3_), channel_id=1, source_target_pairs={{0,1},{1,0},{2,3},{3,2},{4,5},{5,4},{6,7},{7,6},{8,9},{9,8},{10,11... | collective-permute-start | bytes 552968 | tf_op jit(solution)/shard_map/ppermute | solution.py:317
  36.4 4.2 %copy-start.2 = (bf16[3,3,384,96]{2,3,1,0:T(8,128)(2,1)S(1)}, bf16[3,3,384,96]{2,3,1,0:T(8,128)(2,1)}, u32[]{:S(2)}) copy-start(bf16[3,3,384,96]{2,3,1,0:T(8,128)(2,1)} %param.10) | copy-start | bytes 1990660
  36.4 4.2 %copy-start.5 = (f32[96]{0:T(128)S(1)}, f32[96]{0:T(128)}, u32[]{:S(2)}) copy-start(f32[96]{0:T(128)} %param.11) | copy-start | bytes 1156
  40.0 3.4 %collective-permute-start.10 = (bf16[3,224,384]{2,1,0:T(8,128)(2,1)S(1)}, bf16[3,224,384]{2,1,0:T(8,128)(2,1)S(1)}, u32[]{:S(2)}, u32[]{:S(2)}) collective-permute-start(bf16[3,224,384]{2,1,0:T(8,128)(2,1)S(1)} %shard_map.70.refs_0_), channel_id=1, source_target_pairs={{0,1},{1,0},{2,3},{3,2},{4,5},{5,4},{6,7},{7,6},{8,9},{9,8},{10,11... | collective-permute-start | bytes 1548296 | tf_op jit(solution)/shard_map/ppermute | solution.py:317
  40.1 2.1 %collective-permute-start.11 = (bf16[1,224,384]{2,1,0:T(8,128)(2,1)S(1)}, bf16[1,224,384]{2,1,0:T(8,128)(2,1)S(1)}, u32[]{:S(2)}, u32[]{:S(2)}) collective-permute-start(bf16[1,224,384]{2,1,0:T(8,128)(2,1)S(1)} %get-tuple-element.32.refs_0_), channel_id=1, source_target_pairs={{0,1},{1,0},{2,3},{3,2},{4,5},{5,4},{6,7},{7,6},{8,9},{9,8},{10,11... | collective-permute-start | bytes 516104 | tf_op jit(solution)/shard_map/ppermute | solution.py:317
